TPU v7x, 32 devices: a whole 2x2x4 slice. The times are simulated.
32 devices in a mesh: grp: 4 (over x, core), blk: 8 (over z, y).
Axes of the slice: x: 2, y: 2, z: 4, core: 2. Of those that a mesh axis runs over, the one named last changes fastest.
Arguments:
- masses: bfloat16 [8, 2, 256, 256], P('blk'), may hold values from -3 to 3
- spins: int32 [8, 256], P('blk'), may hold values from 0 to 1
- shift_table: int32 [32, 256], P('blk'), may hold values from 0 to 255, as said below
- flip_table: int32 [32, 256], P('blk'), may hold values from 0 to 255, as said below
- ph_in: float32 [2, 32, 256, 256], P(None, 'blk', 'grp'), may hold values from -6 to 6
- pp_in: float32 [2, 32, 256, 256], P(None, 'blk', 'grp'), may hold values from -6 to 6
Outputs:
- ph_out: float32 [2, 32, 256, 256], P(None, 'blk', 'grp')
- pp_out: float32 [2, 32, 256, 256], P(None, 'blk', 'grp')
Inputs may be any that keep to these rules, and one draw needn't show every extreme that they name: Row t of shift_table maps w * 16 + k to ((w + n_t) mod 16) * 16 + (k + q_t) mod 16 for some integers n_t, q_t of the transfer; every row is a permutation. Row t of flip_table maps w * 16 + k to ((n_t - w - 1) mod 16) * 16 + (q_t - k) mod 16 with the same n_t, q_t as shift_table's row t.
All inputs are finite; a program needn't handle non-finite values.
Results may differ from a plain program's by a relative error of at most 0.0064.
Values may be sent and summed in bfloat16 or wider, within the bound.
A program may use at most 128 MiB of HBM per device.

v0:
```python
import functools
import math

import jax
import jax.numpy as jnp
from jax import lax
from jax.experimental import pallas as pl
from jax.experimental.pallas import tpu as pltpu
from jax.sharding import PartitionSpec as P

NW = 16
NK = 16
COUPLING = 0.5
DIRECT = 6
LAG = 2
MESH = pl.DeviceIdType.MESH
NT = (((1,), (1,)), ((), ()))


def angle(steps):
    return steps.astype(jnp.float32) * (math.pi / NW)


def base_steps(row, col):
    return ((2 * (row // NK) + 1) * (col // NK) - 2 * (row % NK) * (col % NK)) % (2 * NW)


def move_steps(freq, mom, col):
    return (2 * freq * (col // NK) - 2 * mom * (col % NK)) % (2 * NW)


def kernel(
    blocks, groups, reach, shift_ref, masses_ref, spins_ref, ph_ref, pp_ref, ph_out, pp_out,
    held, held_spins, col_table, sh_cols, fl_cols, band, sh_rows, fl_rows,
    x_ph, x_pp, fixed, recv_sem, spin_recv, direct_sem, spin_send, core_sem, far_sem, relay_sem,
    local_sem,
):
    group = lax.axis_index("grp")
    block = lax.axis_index("blk")
    order = held.shape[-1]
    walkers = held.shape[1]
    trans = ph_out.shape[1]
    height = order // groups
    chips = groups // 2
    chip, core = group // 2, group % 2
    partner = chip * 2 + (1 - core)
    f32, bf16 = jnp.float32, jnp.bfloat16

    def far(step):
        return lax.rem(chip + step, chips) * 2 + core

    def rows_of(piece):
        return pl.ds(pl.multiple_of(piece * height, height), height)

    gather = reach + 1 == blocks and blocks % 2 == 0 and chips == 2
    layers = blocks // 2
    layer, side = block // 2, block % 2

    def along(offset):
        return lax.rem(layer + offset + layers, layers) * 2 + side

    beside = layer * 2 + (1 - side)
    half = order // 2
    own_rows, far_rows = half * DIRECT // 8, half * (8 - DIRECT) // 8
    own_first = core * half + chip * far_rows
    give_first = core * half + chip * own_rows
    take_first = core * half + (1 - chip) * own_rows
    both_first = core * half + far_rows
    both_rows = own_rows - far_rows
    home = block if gather else 0
    near = [sorted(set(range(layers)) - {one}, key=lambda z: abs(z - one)) for one in range(layers)]

    def near_layer(rank):
        found = 0
        for one in range(layers):
            for i in range(layers - 1):
                hit = jnp.logical_and(layer == one, rank == i)
                found = found + jnp.where(hit, near[one][i], 0)
        return found

    def source_of(step):
        rank = lax.rem(step + 2 * layers - 4, layers - 1)
        direct_side = jnp.where(step <= layers, side, 1 - side)
        found = near_layer(rank) * 2 + direct_side
        return jnp.where(step == 0, block, jnp.where(step == 1, beside, found))

    barrier = pltpu.get_barrier_semaphore()
    if gather:
        sources = [along(offset) for offset in range(1, layers)] + [beside]
    else:
        sources = [lax.rem(block - offset + blocks, blocks) for offset in range(1, reach + 1)]
    for source in sources:
        pl.semaphore_signal(barrier, inc=1, device_id=(group, source), device_id_type=MESH)
    pl.semaphore_signal(barrier, inc=1, device_id=(partner, block), device_id_type=MESH)
    for step in range(1, chips):
        pl.semaphore_signal(barrier, inc=1, device_id=(far(step), block), device_id_type=MESH)

    local = [
        pltpu.make_async_copy(masses_ref, held.at[home], local_sem.at[0]),
        pltpu.make_async_copy(spins_ref, held_spins.at[home], local_sem.at[1]),
        pltpu.make_async_copy(ph_ref, ph_out, local_sem.at[2]),
        pltpu.make_async_copy(pp_ref, pp_out, local_sem.at[3]),
    ]
    for copy in local:
        copy.start()
    pl.semaphore_wait(barrier, len(sources) + chips)

    def direct(offset):
        target = (group, lax.rem(block + offset, blocks))
        return (
            pltpu.make_async_remote_copy(
                src_ref=masses_ref.at[:, :, rows_of(group)],
                dst_ref=held.at[offset, :, :, rows_of(group)],
                send_sem=direct_sem.at[offset, 0],
                recv_sem=recv_sem.at[offset, group],
                device_id=target,
                device_id_type=MESH,
            ),
            pltpu.make_async_remote_copy(
                src_ref=spins_ref,
                dst_ref=held_spins.at[offset],
                send_sem=spin_send.at[offset, 0],
                recv_sem=spin_recv.at[offset],
                device_id=target,
                device_id_type=MESH,
            ),
        )

    def passed(offset, piece, target, send_sem):
        view = held.at[offset, :, :, rows_of(piece)]
        return pltpu.make_async_remote_copy(
            src_ref=view,
            dst_ref=view,
            send_sem=send_sem,
            recv_sem=recv_sem.at[offset, piece],
            device_id=(target, block),
            device_id_type=MESH,
        )

    def to_core(offset):
        return passed(offset, group, partner, core_sem.at[offset, 0])

    def to_far(offset, step):
        return passed(offset, group, far(step), far_sem.at[step, offset])

    def relay(offset, step):
        return passed(offset, far(step), partner, relay_sem.at[step, offset])

    def arrival(offset, piece):
        return passed(offset, piece, partner, core_sem.at[offset, 0])

    def send(src, dst, send_sem, recv, target):
        return pltpu.make_async_remote_copy(
            src_ref=src,
            dst_ref=dst,
            send_sem=send_sem,
            recv_sem=recv,
            device_id=target,
            device_id_type=MESH,
        )

    def block_rows(slot, first, count):
        return held.at[slot, :, :, pl.ds(pl.multiple_of(first, 16), count)]

    def part_of(piece):
        return ((give_first, far_rows), (both_first, both_rows))[piece]

    def hop(slot, target, piece, own):
        first, count = part_of(piece)
        dst = block_rows(slot, first, count)
        src = masses_ref.at[:, :, pl.ds(pl.multiple_of(first, 16), count)] if own else dst
        return send(src, dst, direct_sem.at[slot if not own else target, piece + 2 * own],
                    recv_sem.at[slot, piece], (group, target))

    def note(slot, target, own):
        return send(spins_ref if own else held_spins.at[slot], held_spins.at[slot],
                    spin_send.at[slot if not own else target, 0 + own], spin_recv.at[slot],
                    (group, target))

    def own_hops():
        targets = [beside] + [near_layer(i) * 2 + side for i in range(layers - 1)]
        return [hop(block, target, 0, 1) for target in targets] + [
            copy for target in targets
            for copy in (note(block, target, 1), hop(block, target, 1, 1))
        ]

    def across(slot):
        view = block_rows(slot, give_first, far_rows)
        return send(view, view, far_sem.at[0, slot], recv_sem.at[slot, 2], (far(1), block))

    def taken(slot):
        view = block_rows(slot, take_first, far_rows)
        return send(view, view, far_sem.at[0, slot], recv_sem.at[slot, 2], (far(1), block))

    def share(slot):
        view = block_rows(slot, own_first, own_rows)
        return send(view, view, core_sem.at[slot, 0], recv_sem.at[slot, 3], (partner, block))

    def share_taken(slot):
        view = block_rows(slot, take_first, far_rows)
        return send(view, view, core_sem.at[slot, 1], recv_sem.at[slot, 4], (partner, block))

    if gather:
        for copy in own_hops():
            copy.start()
    else:
        for offset in range(1, reach + 1):
            for copy in direct(offset):
                copy.start()

    norm = 1.0 / math.sqrt(NW * NK)
    index_col = lax.broadcasted_iota(jnp.int32, (order, 128), 0)
    lane = lax.broadcasted_iota(jnp.int32, (order, 128), 1)
    freq = jnp.zeros((order, 128), jnp.int32)
    mom = jnp.zeros((order, 128), jnp.int32)
    for t in range(trans):
        start = shift_ref[t, 0]
        freq = jnp.where(lane == t, start // NK, freq)
        mom = jnp.where(lane == t, start % NK, mom)
    move = angle(move_steps(freq, mom, index_col))
    move_cos, move_sin = jnp.cos(move), jnp.sin(move)

    def put_cols(ref, t, real, imag):
        where = (slice(None),) if t is None else (t, slice(None))
        real, imag = (real * norm).astype(bf16), (imag * norm).astype(bf16)
        ref[where[:-1] + (slice(0, order), slice(0, order))] = real
        ref[where[:-1] + (slice(0, order), slice(order, 2 * order))] = -imag
        ref[where[:-1] + (slice(order, 2 * order), slice(0, order))] = imag
        ref[where[:-1] + (slice(order, 2 * order), slice(order, 2 * order))] = real

    site = lax.broadcasted_iota(jnp.int32, (order, order), 0)
    momentum = lax.broadcasted_iota(jnp.int32, (order, order), 1)
    phase = angle(base_steps(momentum, site))
    cos, sin = jnp.cos(phase), jnp.sin(phase)
    put_cols(col_table, None, cos, sin)
    for t in range(trans):
        mc, ms = move_cos[:, t : t + 1], move_sin[:, t : t + 1]
        cc, ss, sc, cs = mc * cos, ms * sin, ms * cos, mc * sin
        put_cols(sh_cols, t, cc - ss, sc + cs)
        put_cols(fl_cols, t, cc + ss, sc - cs)

    row = lax.broadcasted_iota(jnp.int32, (height, order), 0) + group * height
    column = lax.broadcasted_iota(jnp.int32, (height, order), 1)
    phase = angle(base_steps(row, column))
    cos, sin = jnp.cos(phase), jnp.sin(phase)
    band[0:height, :] = (cos * norm).astype(bf16)
    band[height : 2 * height, :] = (sin * norm).astype(bf16)
    col8 = lax.broadcasted_iota(jnp.int32, (8, order), 1)
    for t in range(trans):
        start = shift_ref[t, 0]
        move = angle(move_steps(start // NK, start % NK, col8))
        mc, ms = jnp.cos(move)[0:1], jnp.sin(move)[0:1]
        cc, ss, sc, cs = mc * cos, ms * sin, ms * cos, mc * sin
        first = 2 * t * height
        sh_rows[first : first + height, :] = ((cc - ss) * norm).astype(bf16)
        sh_rows[first + height : first + 2 * height, :] = ((sc + cs) * norm).astype(bf16)
        fl_rows[first : first + height, :] = ((cc + ss) * norm).astype(bf16)
        fl_rows[first + height : first + 2 * height, :] = ((sc - cs) * norm).astype(bf16)

    def dot(a, b):
        return jnp.dot(a, b, preferred_element_type=f32)

    def absorb(slot):
        for w in range(walkers):
            place = pl.ds(pl.multiple_of((slot * walkers + w) * height, height), height)
            signed = (2 * held_spins[slot, w : w + 1, :] - 1).astype(f32)
            lefts = []
            for s in range(2):
                factor = jnp.exp((COUPLING if s == 0 else -COUPLING) * signed)
                scaled = (held[slot, w, s].astype(f32) * factor).astype(bf16)
                moved = dot(sh_rows[...], scaled).astype(bf16)
                for t in range(trans):
                    first = 2 * t * height
                    x_ph[t, s, place, 0:order] = moved[first : first + height]
                    x_ph[t, s, place, order:] = moved[first + height : first + 2 * height]
                if s == 1:
                    moved = dot(fl_rows[...], scaled).astype(bf16)
                    for t in range(trans):
                        first = 2 * t * height
                        x_pp[t, place, 0:order] = moved[first : first + height]
                        x_pp[t, place, order:] = moved[first + height : first + 2 * height]
                else:
                    upper = dot(band[...], scaled).astype(bf16)
                left = lax.dot_general(band[...], scaled, NT, preferred_element_type=f32)
                lefts.append(left.astype(bf16))
            lefts.append(upper)
            joined = jnp.concatenate(
                [jnp.concatenate([one[:height], one[height:]], 1) for one in lefts], 0
            )
            second = dot(joined, col_table[...])
            for part in range(3):
                fixed[part, place, :] = second[part * height : (part + 1) * height]

    if gather:

        @pl.loop(0, reach + LAG + 2)
        def _(k):
            @pl.when(jnp.logical_and(k >= 1, k <= reach))
            def _():
                slot = source_of(k)
                hop(slot, beside, 0, 0).wait_recv()
                across(slot).start()

                @pl.when(jnp.logical_and(k >= 2, k <= layers))
                def _():
                    hop(slot, beside, 0, 0).start()

            @pl.when(jnp.logical_and(k >= LAG + 1, k <= reach + LAG))
            def _():
                slot = source_of(k - LAG)
                hop(slot, beside, 1, 0).wait_recv()
                note(slot, beside, 0).wait_recv()

                @pl.when(jnp.logical_and(k >= LAG + 2, k <= layers + LAG))
                def _():
                    hop(slot, beside, 1, 0).start()
                    note(slot, beside, 0).start()

                share(slot).start()
                taken(slot).wait_recv()
                share_taken(slot).start()

            @pl.when(k == LAG + 1)
            def _():
                local[0].wait()
                local[1].wait()

            @pl.when(k >= LAG + 2)
            def _():
                slot = source_of(k - LAG - 1)
                share(slot).wait_recv()
                share_taken(slot).wait_recv()

            @pl.when(k >= LAG + 1)
            def _():
                absorb(source_of(k - LAG - 1))

    else:

        @pl.loop(0, reach + 3)
        def _(k):
            @pl.when(jnp.logical_and(k >= 1, k <= reach))
            def _():
                arrival(k, group).wait_recv()
                for step in range(1, chips):
                    to_far(k, step).start()
                to_core(k).start()

            @pl.when(jnp.logical_and(k >= 2, k <= reach + 1))
            def _():
                for step in range(1, chips):
                    arrival(k - 1, far(step)).wait_recv()
                    relay(k - 1, step).start()

            @pl.when(k == 2)
            def _():
                local[0].wait()
                local[1].wait()

            @pl.when(k >= 3)
            def _():
                arrival(k - 2, partner).wait_recv()
                for step in range(1, chips):
                    piece = lax.rem(chip + step, chips) * 2 + (1 - core)
                    arrival(k - 2, piece).wait_recv()
                direct(k - 2)[1].wait_recv()

            @pl.when(k >= 2)
            def _():
                absorb(k - 2)

    local[2].wait()
    local[3].wait()
    length = (reach + 1) * walkers

    def product(left, right):
        for v in range(length):
            part = slice(v * height, (v + 1) * height)
            a, b = left[part, 0:order], left[part, order:]
            c, d = right[part, 0:order], right[part, order:]
            yield a, b, c, d

    @pl.loop(0, trans)
    def _(t):
        real, imag = ph_out[0, t], ph_out[1, t]
        for s in range(2):
            moved = dot(x_ph[t, s], sh_cols[t])
            for a, b, c, d in product(fixed[s], moved):
                real = real + (a * c + b * d)
                imag = imag + (a * d - b * c)
        ph_out[0, t] = real
        ph_out[1, t] = imag
        real, imag = pp_out[0, t], pp_out[1, t]
        lowered = dot(x_pp[t], fl_cols[t])
        for a, b, c, d in product(fixed[2], lowered):
            real = real + (a * c - b * d)
            imag = imag + (a * d + b * c)
        pp_out[0, t] = real
        pp_out[1, t] = imag

    if gather:
        for copy in own_hops():
            copy.wait_send()
        for step in range(1, reach + 1):
            slot = source_of(step)
            if 2 <= step <= layers:
                hop(slot, beside, 0, 0).wait_send()
                hop(slot, beside, 1, 0).wait_send()
                note(slot, beside, 0).wait_send()
            across(slot).wait_send()
            share(slot).wait_send()
            share_taken(slot).wait_send()
    else:
        for offset in range(1, reach + 1):
            for copy in direct(offset):
                copy.wait_send()
            to_core(offset).wait_send()
            for step in range(1, chips):
                to_far(offset, step).wait_send()
                relay(offset, step).wait_send()


def on_device(masses, spins, shift_table, flip_table, ph_in, pp_in):
    groups = lax.axis_size("grp")
    blocks = lax.axis_size("blk")
    reach = min(8, blocks - 1)
    visits = reach + 1
    walkers, _, order, _ = masses.shape
    trans = shift_table.shape[0]
    height = order // groups
    chips = groups // 2
    f32, bf16 = jnp.float32, jnp.bfloat16
    dma = pltpu.SemaphoreType.DMA
    anywhere = pl.BlockSpec(memory_space=pl.ANY)
    return pl.pallas_call(
        functools.partial(kernel, blocks, groups, reach),
        out_shape=(
            jax.ShapeDtypeStruct(ph_in.shape, f32),
            jax.ShapeDtypeStruct(pp_in.shape, f32),
        ),
        in_specs=[pl.BlockSpec(memory_space=pltpu.SMEM)] + [anywhere] * 4,
        out_specs=(pl.BlockSpec(memory_space=pltpu.VMEM),) * 2,
        scratch_shapes=[
            pltpu.VMEM((visits, walkers, 2, order, order), bf16),
            pltpu.VMEM((visits, walkers, order), jnp.int32),
            pltpu.VMEM((2 * order, 2 * order), bf16),
            pltpu.VMEM((trans, 2 * order, 2 * order), bf16),
            pltpu.VMEM((trans, 2 * order, 2 * order), bf16),
            pltpu.VMEM((2 * height, order), bf16),
            pltpu.VMEM((trans * 2 * height, order), bf16),
            pltpu.VMEM((trans * 2 * height, order), bf16),
            pltpu.VMEM((trans, 2, visits * walkers * height, 2 * order), bf16),
            pltpu.VMEM((trans, visits * walkers * height, 2 * order), bf16),
            pltpu.VMEM((3, visits * walkers * height, 2 * order), f32),
            dma((visits, max(groups, 5))),
            dma((visits,)),
            dma((visits, 4)),
            dma((visits, 2)),
            dma((visits, 2)),
            dma((chips, visits)),
            dma((chips, visits)),
            dma((4,)),
        ],
        compiler_params=pltpu.CompilerParams(
            collective_id=0, has_side_effects=True, vmem_limit_bytes=56 * 1024 * 1024
        ),
    )(shift_table, masses, spins, ph_in, pp_in)


def solution(mesh):
    placed = (
        P("blk", None, None, None),
        P("blk", None),
        P("blk", None),
        P("blk", None),
        P(None, "blk", "grp", None),
        P(None, "blk", "grp", None),
    )
    return jax.shard_map(
        on_device,
        mesh=mesh,
        in_specs=placed,
        out_specs=(P(None, "blk", "grp", None), P(None, "blk", "grp", None)),
        check_vma=False,
    )
```

profile of v0, /device:TPU:0, one launch (start us, length us, event | category | flops | bytes accessed | tf_op | source)
XLA Modules:
  0.0 31.7 jit_solution(9787072367025975259)
XLA Ops:
  0.6 28.4 %shard_map.68 = (f32[2,4,64,256]{3,2,1,0:T(8,128)}, f32[2,4,64,256]{3,2,1,0:T(8,128)}) custom-call(s32[4,256]{1,0:T(4,128)} %shift_ref.1, bf16[1,2,256,256]{3,2,1,0:T(8,128)(2,1)} %masses_ref.1, s32[1,256]{1,0:T(1,128)} %spins_ref.1, f32[2,4,64,256]{3,2,1,0:T(8,128)} %ph_ref.1, f32[2,4,64,256]{3,2,1,0:T(8,128)} %pp_ref.1), custom_call_target="tpu_custom_call" | custom-call | tf_op jit(solution)/shard_map/pallas_call | solution.py:435
  29.0 0.0 copy-start
  29.0 1.9 %copy.9 = f32[2,4,64,256]{3,2,1,0:T(8,128)} copy(f32[2,4,64,256]{3,2,1,0:T(8,128)} %get-tuple-element.4) | data formatting | bytes 1048576
  30.9 0.0 copy-done
  31.0 0.8 %copy.10 = f32[2,4,64,256]{3,2,1,0:T(8,128)} copy(f32[2,4,64,256]{3,2,1,0:T(8,128)S(1)} %copy-done) | data formatting | bytes 1048576
Async XLA Ops:
  29.0 1.9 %copy-start = (f32[2,4,64,256]{3,2,1,0:T(8,128)S(1)}, f32[2,4,64,256]{3,2,1,0:T(8,128)}, u32[]{:S(2)}) copy-start(f32[2,4,64,256]{3,2,1,0:T(8,128)} %get-tuple-element.5) | copy-start | bytes 1572868
where the time goes:
time: 31.9 us; the launch traced here: 31.7 us
  Pallas kernels  28.4 us (89%)
  local copies, waits for them, and re-layouts  2.72 us (9%)
  between operations  0.65 us (2%)
    pallas_call x1, Pallas kernels, on_device(): pl.pallas_call(functools.partial(kernel, blocks, groups, reach), out_shap...  28.4 us
    unnamed x4, local copies, waits for them, and re-layouts  2.72 us

commit v1 on v0

v1 whole, which is shorter than its diff:
```python
import functools
import math

import jax
import jax.numpy as jnp
from jax import lax
from jax.experimental import pallas as pl
from jax.experimental.pallas import tpu as pltpu
from jax.sharding import PartitionSpec as P

NW = 16
NK = 16
COUPLING = 0.5
MESH = pl.DeviceIdType.MESH
NT = (((1,), (1,)), ((), ()))


def angle(steps):
    return steps.astype(jnp.float32) * (math.pi / NW)


def base_steps(row, col):
    return ((2 * (row // NK) + 1) * (col // NK) - 2 * (row % NK) * (col % NK)) % (2 * NW)


def move_steps(freq, mom, col):
    return (2 * freq * (col // NK) - 2 * mom * (col % NK)) % (2 * NW)


def whole_gather(blocks, groups, reach):
    return blocks == 8 and groups == 4 and reach == 7


def send(src, dst, send_sem, recv_sem, target):
    return pltpu.make_async_remote_copy(
        src_ref=src,
        dst_ref=dst,
        send_sem=send_sem,
        recv_sem=recv_sem,
        device_id=target,
        device_id_type=MESH,
    )


def bulk(view, sem):
    return pltpu.make_async_copy(view, view, sem)


class Gather:
    TURNS = ("", "O0 O1 H0 I0", "H1 h0 F0", "F1 i0 I1", "h1 f0", "f1 i1", "", "")
    SLOTS = "SOHFIhfi"

    def __init__(self, group, block, order, walkers, masses, spins, held, held_spins, recv, sends):
        self.chip, self.core = group // 2, group % 2
        self.block, self.layer, self.side = block, block // 2, block % 2
        self.masses, self.spins = masses, spins
        self.held, self.held_spins = held, held_spins
        self.recv, self.sends = recv, sends
        self.quarter = order // 4
        self.walkers = walkers
        self.end = jnp.logical_or(self.layer == 0, self.layer == 3)
        other = self.chip * 2 + (1 - self.core)
        self.other = other
        self.partner = (other, block)
        self.across = ((1 - self.chip) * 2 + (1 - self.core), block)
        self.beside = (other, self.layer * 2 + (1 - self.side))
        same, mate = self.side, 1 - self.side
        first, second = self.by_layer(1, 3, 0, 2), self.by_layer(2, 2, 1, 1)
        full = self.by_layer(3, 0, 3, 0)
        self.slots = {
            "S": block,
            "O": self.layer * 2 + mate,
            "H": first * 2 + same,
            "I": second * 2 + same,
            "F": full * 2 + same,
            "h": first * 2 + mate,
            "i": second * 2 + mate,
            "f": full * 2 + mate,
        }

    def by_layer(self, *values):
        return sum(
            value * (self.layer == i).astype(jnp.int32) for i, value in enumerate(values)
        )

    def slot_at(self, k):
        return sum(
            self.slots[kind] * (k == i).astype(jnp.int32) for i, kind in enumerate(self.SLOTS)
        )

    def up(self, layer):
        return (self.other, layer * 2 + self.side)

    def others(self):
        return [(self.other, lax.rem(self.block + step, 8)) for step in range(1, 8)]

    def greet(self):
        self.barrier = pltpu.get_barrier_semaphore()
        targets = self.others() + [self.partner, self.across]
        for target in targets:
            pl.semaphore_signal(self.barrier, inc=1, device_id=target, device_id_type=MESH)

    def enter(self):
        pl.semaphore_wait(self.barrier, 9)

    def rows(self, ref, half, parity):
        first = pl.multiple_of((half * 2 + parity) * self.quarter, self.quarter)
        return ref.at[:, :, pl.ds(first, self.quarter)]

    def own(self, part, target):
        half = 1 - self.chip if part else self.chip
        dst = self.rows(self.held.at[self.block], half, 1 - self.core)
        src = self.rows(self.masses, half, 1 - self.core)
        send(src, dst, self.sends.at[0], self.recv.at[self.block, part], target).start()

    def note(self, target):
        return send(self.spins, self.held_spins.at[self.block], self.sends.at[3],
                    self.sends.at[4], target)

    def begin(self):
        for target in self.others():
            self.note(target).start()
        ends = self.by_layer(1, 0, 0, 2), self.by_layer(3, 0, 0, 0)
        inner = self.by_layer(2, 2, 1, 1)
        near_end, far_end = self.by_layer(0, 0, 3, 0), self.by_layer(0, 3, 0, 0)

        @pl.when(self.end)
        def _():
            self.own(0, self.beside)
            self.own(1, self.beside)
            self.own(0, self.up(inner))
            for layer in ends:
                self.own(0, self.up(layer))
                self.own(1, self.up(layer))

        @pl.when(jnp.logical_not(self.end))
        def _():
            self.own(0, self.up(near_end))
            self.own(0, self.up(far_end))
            self.own(0, self.beside)
            self.own(1, self.beside)
            self.own(0, self.up(inner))

    def parity(self, kind, part):
        moved = kind in "fi" if part == 0 else kind in "HIf"
        if kind == "h":
            moved = part == 0
        return 1 - self.core if moved else self.core

    def event(self, kind, part):
        slot = self.slots[kind]
        half = 1 - self.chip if part else self.chip
        view = self.rows(self.held.at[slot], half, self.parity(kind, part))

        def copy(sem, recv, target):
            return send(view, view, self.sends.at[sem], self.recv.at[slot, recv], target)

        copy(1, part, self.partner).wait_recv()
        if kind == "F" or (kind in "HI" and part == 0):
            copy(1, part, self.beside).start()
        if kind in "HIhi" and part == 0:
            copy(1, 1, self.across).start()
        copy(2, 2, self.partner).start()

    def some(self, count):
        return self.held.at[0:count, :, :, 0 : self.quarter]

    def turn(self, k):
        for i, turn in enumerate(self.TURNS):
            if turn:
                @pl.when(k == i)
                def _():
                    for name in turn.split():
                        self.event(name[0], int(name[1]))

        @pl.when(k == 1)
        def _():
            bulk(self.held_spins.at[0:7], self.sends.at[4]).wait()

        @pl.when(k >= 1)
        def _():
            half = self.held.at[0, :, :, 0 : 2 * self.quarter]
            bulk(half, self.recv.at[self.slot_at(k), 2]).wait()

    def drain(self):
        pl.when(self.end)(lambda: bulk(self.some(7), self.sends.at[0]).wait())
        pl.when(jnp.logical_not(self.end))(lambda: bulk(self.some(5), self.sends.at[0]).wait())
        bulk(self.some(8), self.sends.at[1]).wait()
        bulk(self.held.at[0:7, :, :, 0 : 2 * self.quarter], self.sends.at[2]).wait()
        bulk(self.held_spins.at[0:7], self.sends.at[3]).wait()


class Chain:
    def __init__(self, group, block, groups, blocks, reach, height, masses, spins, held,
                 held_spins, recv, sends):
        self.group, self.block = group, block
        self.blocks, self.reach, self.height = blocks, reach, height
        self.groups, self.chips = groups, groups // 2
        self.chip, self.core = group // 2, group % 2
        self.partner = self.chip * 2 + (1 - self.core)
        self.masses, self.spins = masses, spins
        self.held, self.held_spins = held, held_spins
        self.recv, self.sends = recv, sends

    def slot_at(self, k):
        return k

    def far(self, step):
        return lax.rem(self.chip + step, self.chips) * 2 + self.core

    def rows(self, ref, piece):
        first = pl.multiple_of(piece * self.height, self.height)
        return ref.at[:, :, pl.ds(first, self.height)]

    def greet(self):
        self.barrier = pltpu.get_barrier_semaphore()
        blocks = [
            lax.rem(self.block - offset + self.blocks, self.blocks)
            for offset in range(1, self.reach + 1)
        ]
        targets = [(self.group, block) for block in blocks] + [(self.partner, self.block)]
        targets += [(self.far(step), self.block) for step in range(1, self.chips)]
        for target in targets:
            pl.semaphore_signal(self.barrier, inc=1, device_id=target, device_id_type=MESH)

    def enter(self):
        pl.semaphore_wait(self.barrier, self.reach + self.chips)

    def direct(self, offset):
        target = (self.group, lax.rem(self.block + offset, self.blocks))
        return (
            send(
                self.rows(self.masses, self.group),
                self.rows(self.held.at[offset], self.group),
                self.sends.at[offset, 0], self.recv.at[offset, self.group], target,
            ),
            send(
                self.spins, self.held_spins.at[offset],
                self.sends.at[offset, 1], self.recv.at[offset, self.groups], target,
            ),
        )

    def passed(self, offset, piece, target, sem):
        view = self.rows(self.held.at[offset], piece)
        return send(view, view, self.sends.at[offset, sem], self.recv.at[offset, piece],
                    (target, self.block))

    def to_core(self, offset):
        return self.passed(offset, self.group, self.partner, 2)

    def to_far(self, offset, step):
        return self.passed(offset, self.group, self.far(step), 1 + 2 * step)

    def relay(self, offset, step):
        return self.passed(offset, self.far(step), self.partner, 2 + 2 * step)

    def arrival(self, offset, piece):
        return self.passed(offset, piece, self.partner, 2)

    def begin(self):
        for offset in range(1, self.reach + 1):
            for copy in self.direct(offset):
                copy.start()

    def take(self, k):
        self.arrival(k, self.group).wait_recv()
        for step in range(1, self.chips):
            self.to_far(k, step).start()
        self.to_core(k).start()

    def turn(self, k):
        pl.when(k == 0)(lambda: self.take(1))
        pl.when(jnp.logical_and(k >= 1, k < self.reach))(lambda: self.take(k + 1))

        @pl.when(k >= 1)
        def _():
            for step in range(1, self.chips):
                self.arrival(k, self.far(step)).wait_recv()
                self.relay(k, step).start()
            self.arrival(k, self.partner).wait_recv()
            for step in range(1, self.chips):
                piece = lax.rem(self.chip + step, self.chips) * 2 + (1 - self.core)
                self.arrival(k, piece).wait_recv()
            self.direct(k)[1].wait_recv()

    def drain(self):
        for offset in range(1, self.reach + 1):
            for copy in self.direct(offset):
                copy.wait_send()
            self.to_core(offset).wait_send()
            for step in range(1, self.chips):
                self.to_far(offset, step).wait_send()
                self.relay(offset, step).wait_send()

def kernel(
    blocks, groups, reach, shift_ref, masses_ref, spins_ref, ph_ref, pp_ref, ph_out, pp_out,
    held, held_spins, col_table, sh_cols, fl_cols, band, sh_rows, fl_rows,
    x_ph, x_pp, fixed, recv_sem, send_sem, local_sem,
):
    group = lax.axis_index("grp")
    block = lax.axis_index("blk")
    order = held.shape[-1]
    walkers = held.shape[1]
    trans = ph_out.shape[1]
    height = order // groups
    chips = groups // 2
    chip, core = group // 2, group % 2
    partner = chip * 2 + (1 - core)
    f32, bf16 = jnp.float32, jnp.bfloat16
    gather = whole_gather(blocks, groups, reach)
    home = block if gather else 0

    local = [
        pltpu.make_async_copy(masses_ref, held.at[home], local_sem.at[0]),
        pltpu.make_async_copy(spins_ref, held_spins.at[home], local_sem.at[1]),
        pltpu.make_async_copy(ph_ref, ph_out, local_sem.at[2]),
        pltpu.make_async_copy(pp_ref, pp_out, local_sem.at[3]),
    ]
    if gather:
        plan = Gather(
            group, block, order, walkers, masses_ref, spins_ref, held, held_spins,
            recv_sem, send_sem,
        )
    else:
        plan = Chain(
            group, block, groups, blocks, reach, height, masses_ref, spins_ref, held,
            held_spins, recv_sem, send_sem,
        )
    plan.greet()
    for copy in local:
        copy.start()
    plan.enter()
    plan.begin()

    norm = 1.0 / math.sqrt(NW * NK)
    index_col = lax.broadcasted_iota(jnp.int32, (order, 128), 0)
    lane = lax.broadcasted_iota(jnp.int32, (order, 128), 1)
    freq = jnp.zeros((order, 128), jnp.int32)
    mom = jnp.zeros((order, 128), jnp.int32)
    for t in range(trans):
        start = shift_ref[t, 0]
        freq = jnp.where(lane == t, start // NK, freq)
        mom = jnp.where(lane == t, start % NK, mom)
    move = angle(move_steps(freq, mom, index_col))
    move_cos, move_sin = jnp.cos(move), jnp.sin(move)

    def put_cols(ref, t, real, imag):
        where = (slice(None),) if t is None else (t, slice(None))
        real, imag = (real * norm).astype(bf16), (imag * norm).astype(bf16)
        ref[where[:-1] + (slice(0, order), slice(0, order))] = real
        ref[where[:-1] + (slice(0, order), slice(order, 2 * order))] = -imag
        ref[where[:-1] + (slice(order, 2 * order), slice(0, order))] = imag
        ref[where[:-1] + (slice(order, 2 * order), slice(order, 2 * order))] = real

    site = lax.broadcasted_iota(jnp.int32, (order, order), 0)
    momentum = lax.broadcasted_iota(jnp.int32, (order, order), 1)
    phase = angle(base_steps(momentum, site))
    cos, sin = jnp.cos(phase), jnp.sin(phase)
    put_cols(col_table, None, cos, sin)
    for t in range(trans):
        mc, ms = move_cos[:, t : t + 1], move_sin[:, t : t + 1]
        cc, ss, sc, cs = mc * cos, ms * sin, ms * cos, mc * sin
        put_cols(sh_cols, t, cc - ss, sc + cs)
        put_cols(fl_cols, t, cc + ss, sc - cs)

    row = lax.broadcasted_iota(jnp.int32, (height, order), 0) + group * height
    column = lax.broadcasted_iota(jnp.int32, (height, order), 1)
    phase = angle(base_steps(row, column))
    cos, sin = jnp.cos(phase), jnp.sin(phase)
    band[0:height, :] = (cos * norm).astype(bf16)
    band[height : 2 * height, :] = (sin * norm).astype(bf16)
    col8 = lax.broadcasted_iota(jnp.int32, (8, order), 1)
    for t in range(trans):
        start = shift_ref[t, 0]
        move = angle(move_steps(start // NK, start % NK, col8))
        mc, ms = jnp.cos(move)[0:1], jnp.sin(move)[0:1]
        cc, ss, sc, cs = mc * cos, ms * sin, ms * cos, mc * sin
        first = 2 * t * height
        sh_rows[first : first + height, :] = ((cc - ss) * norm).astype(bf16)
        sh_rows[first + height : first + 2 * height, :] = ((sc + cs) * norm).astype(bf16)
        fl_rows[first : first + height, :] = ((cc + ss) * norm).astype(bf16)
        fl_rows[first + height : first + 2 * height, :] = ((sc - cs) * norm).astype(bf16)

    def dot(a, b):
        return jnp.dot(a, b, preferred_element_type=f32)

    def absorb(slot):
        for w in range(walkers):
            place = pl.ds(pl.multiple_of((slot * walkers + w) * height, height), height)
            signed = (2 * held_spins[slot, w : w + 1, :] - 1).astype(f32)
            lefts = []
            for s in range(2):
                factor = jnp.exp((COUPLING if s == 0 else -COUPLING) * signed)
                scaled = (held[slot, w, s].astype(f32) * factor).astype(bf16)
                moved = dot(sh_rows[...], scaled).astype(bf16)
                for t in range(trans):
                    first = 2 * t * height
                    x_ph[t, s, place, 0:order] = moved[first : first + height]
                    x_ph[t, s, place, order:] = moved[first + height : first + 2 * height]
                if s == 1:
                    moved = dot(fl_rows[...], scaled).astype(bf16)
                    for t in range(trans):
                        first = 2 * t * height
                        x_pp[t, place, 0:order] = moved[first : first + height]
                        x_pp[t, place, order:] = moved[first + height : first + 2 * height]
                else:
                    upper = dot(band[...], scaled).astype(bf16)
                left = lax.dot_general(band[...], scaled, NT, preferred_element_type=f32)
                lefts.append(left.astype(bf16))
            lefts.append(upper)
            joined = jnp.concatenate(
                [jnp.concatenate([one[:height], one[height:]], 1) for one in lefts], 0
            )
            second = dot(joined, col_table[...])
            for part in range(3):
                fixed[part, place, :] = second[part * height : (part + 1) * height]

    @pl.loop(0, reach + 1)
    def _(k):
        @pl.when(k == 0)
        def _():
            local[0].wait()
            local[1].wait()

        plan.turn(k)
        absorb(plan.slot_at(k))

    local[2].wait()
    local[3].wait()
    length = (reach + 1) * walkers

    def product(left, right):
        for v in range(length):
            part = slice(v * height, (v + 1) * height)
            a, b = left[part, 0:order], left[part, order:]
            c, d = right[part, 0:order], right[part, order:]
            yield a, b, c, d

    @pl.loop(0, trans)
    def _(t):
        real, imag = ph_out[0, t], ph_out[1, t]
        for s in range(2):
            moved = dot(x_ph[t, s], sh_cols[t])
            for a, b, c, d in product(fixed[s], moved):
                real = real + (a * c + b * d)
                imag = imag + (a * d - b * c)
        ph_out[0, t] = real
        ph_out[1, t] = imag
        real, imag = pp_out[0, t], pp_out[1, t]
        lowered = dot(x_pp[t], fl_cols[t])
        for a, b, c, d in product(fixed[2], lowered):
            real = real + (a * c - b * d)
            imag = imag + (a * d + b * c)
        pp_out[0, t] = real
        pp_out[1, t] = imag

    plan.drain()


def on_device(masses, spins, shift_table, flip_table, ph_in, pp_in):
    groups = lax.axis_size("grp")
    blocks = lax.axis_size("blk")
    reach = min(8, blocks - 1)
    visits = reach + 1
    walkers, _, order, _ = masses.shape
    trans = shift_table.shape[0]
    height = order // groups
    chips = groups // 2
    f32, bf16 = jnp.float32, jnp.bfloat16
    dma = pltpu.SemaphoreType.DMA
    anywhere = pl.BlockSpec(memory_space=pl.ANY)
    if whole_gather(blocks, groups, reach):
        recv_shape, send_shape = (visits, 3), (5,)
    else:
        recv_shape, send_shape = (visits, groups + 1), (visits, 3 + 2 * (chips - 1))
    return pl.pallas_call(
        functools.partial(kernel, blocks, groups, reach),
        out_shape=(
            jax.ShapeDtypeStruct(ph_in.shape, f32),
            jax.ShapeDtypeStruct(pp_in.shape, f32),
        ),
        in_specs=[pl.BlockSpec(memory_space=pltpu.SMEM)] + [anywhere] * 4,
        out_specs=(pl.BlockSpec(memory_space=pltpu.VMEM),) * 2,
        scratch_shapes=[
            pltpu.VMEM((visits, walkers, 2, order, order), bf16),
            pltpu.VMEM((visits, walkers, order), jnp.int32),
            pltpu.VMEM((2 * order, 2 * order), bf16),
            pltpu.VMEM((trans, 2 * order, 2 * order), bf16),
            pltpu.VMEM((trans, 2 * order, 2 * order), bf16),
            pltpu.VMEM((2 * height, order), bf16),
            pltpu.VMEM((trans * 2 * height, order), bf16),
            pltpu.VMEM((trans * 2 * height, order), bf16),
            pltpu.VMEM((trans, 2, visits * walkers * height, 2 * order), bf16),
            pltpu.VMEM((trans, visits * walkers * height, 2 * order), bf16),
            pltpu.VMEM((3, visits * walkers * height, 2 * order), f32),
            dma(recv_shape),
            dma(send_shape),
            dma((4,)),
        ],
        compiler_params=pltpu.CompilerParams(
            collective_id=0, has_side_effects=True, vmem_limit_bytes=56 * 1024 * 1024
        ),
    )(shift_table, masses, spins, ph_in, pp_in)


def solution(mesh):
    placed = (
        P("blk", None, None, None),
        P("blk", None),
        P("blk", None),
        P("blk", None),
        P(None, "blk", "grp", None),
        P(None, "blk", "grp", None),
    )
    return jax.shard_map(
        on_device,
        mesh=mesh,
        in_specs=placed,
        out_specs=(P(None, "blk", "grp", None), P(None, "blk", "grp", None)),
        check_vma=False,
    )
```

time: 31.9 us -> 32 us (level)
  no operation moved by 1% of the time
where the time goes in v1:
time: 32 us; the launch traced here: 31.8 us
  Pallas kernels  28.4 us (89%)
  local copies, waits for them, and re-layouts  2.72 us (8%)
  between operations  0.65 us (2%)
    pallas_call x1, Pallas kernels, on_device(): pl.pallas_call(functools.partial(kernel, blocks, groups, reach), out_shap...  28.4 us
    unnamed x4, local copies, waits for them, and re-layouts  2.72 us

profile of v1, /device:TPU:0, one launch (start us, length us, event | category | flops | bytes accessed | tf_op | source)
XLA Modules:
  0.0 31.8 jit_solution(7538245987429703063)
XLA Ops:
  0.6 28.4 %shard_map.68 = (f32[2,4,64,256]{3,2,1,0:T(8,128)}, f32[2,4,64,256]{3,2,1,0:T(8,128)}) custom-call(s32[4,256]{1,0:T(4,128)} %shift_ref.1, bf16[1,2,256,256]{3,2,1,0:T(8,128)(2,1)} %masses_ref.1, s32[1,256]{1,0:T(1,128)} %spins_ref.1, f32[2,4,64,256]{3,2,1,0:T(8,128)} %ph_ref.1, f32[2,4,64,256]{3,2,1,0:T(8,128)} %pp_ref.1), custom_call_target="tpu_custom_call" | custom-call | tf_op jit(solution)/shard_map/pallas_call | solution.py:476
  29.0 0.0 copy-start
  29.1 1.9 %copy.9 = f32[2,4,64,256]{3,2,1,0:T(8,128)} copy(f32[2,4,64,256]{3,2,1,0:T(8,128)} %get-tuple-element.4) | data formatting | bytes 1048576
  31.0 0.0 copy-done
  31.0 0.8 %copy.10 = f32[2,4,64,256]{3,2,1,0:T(8,128)} copy(f32[2,4,64,256]{3,2,1,0:T(8,128)S(1)} %copy-done) | data formatting | bytes 1048576
Async XLA Ops:
  29.0 1.9 %copy-start = (f32[2,4,64,256]{3,2,1,0:T(8,128)S(1)}, f32[2,4,64,256]{3,2,1,0:T(8,128)}, u32[]{:S(2)}) copy-start(f32[2,4,64,256]{3,2,1,0:T(8,128)} %get-tuple-element.5) | copy-start | bytes 1572868

commit v2 on v1

--- a/solution.py
+++ b/solution.py
@@ -11,6 +11,7 @@
 NW = 16
 NK = 16
 COUPLING = 0.5
+VMEM = 67043328
 MESH = pl.DeviceIdType.MESH
 NT = (((1,), (1,)), ((), ()))
 
@@ -457,6 +458,17 @@
     plan.drain()
 
 
+def leave(ph_sum, pp_sum, ph_out, pp_out, sem):
+    copies = [
+        pltpu.make_async_copy(ph_sum, ph_out, sem.at[0]),
+        pltpu.make_async_copy(pp_sum, pp_out, sem.at[1]),
+    ]
+    for copy in copies:
+        copy.start()
+    for copy in copies:
+        copy.wait()
+
+
 def on_device(masses, spins, shift_table, flip_table, ph_in, pp_in):
     groups = lax.axis_size("grp")
     blocks = lax.axis_size("blk")
@@ -473,13 +485,11 @@
         recv_shape, send_shape = (visits, 3), (5,)
     else:
         recv_shape, send_shape = (visits, groups + 1), (visits, 3 + 2 * (chips - 1))
-    return pl.pallas_call(
+    sums = pl.pallas_call(
         functools.partial(kernel, blocks, groups, reach),
-        out_shape=(
-            jax.ShapeDtypeStruct(ph_in.shape, f32),
-            jax.ShapeDtypeStruct(pp_in.shape, f32),
-        ),
-        in_specs=[pl.BlockSpec(memory_space=pltpu.SMEM)] + [anywhere] * 4,
+        out_shape=(pltpu.VMEM(ph_in.shape, f32), pltpu.VMEM(pp_in.shape, f32)),
+        in_specs=[pl.BlockSpec(memory_space=pltpu.SMEM)]
+        + [pl.BlockSpec(memory_space=pltpu.HBM)] * 4,
         out_specs=(pl.BlockSpec(memory_space=pltpu.VMEM),) * 2,
         scratch_shapes=[
             pltpu.VMEM((visits, walkers, 2, order, order), bf16),
@@ -498,9 +508,19 @@
             dma((4,)),
         ],
         compiler_params=pltpu.CompilerParams(
-            collective_id=0, has_side_effects=True, vmem_limit_bytes=56 * 1024 * 1024
+            collective_id=0, has_side_effects=True, vmem_limit_bytes=VMEM - 4 * (ph_in.size + pp_in.size) - 65536
         ),
     )(shift_table, masses, spins, ph_in, pp_in)
+    return pl.pallas_call(
+        leave,
+        out_shape=(
+            jax.ShapeDtypeStruct(ph_in.shape, f32),
+            jax.ShapeDtypeStruct(pp_in.shape, f32),
+        ),
+        in_specs=[pl.BlockSpec(memory_space=pltpu.VMEM)] * 2,
+        out_specs=(anywhere,) * 2,
+        scratch_shapes=[dma((2,))],
+    )(*[pltpu.with_memory_space_constraint(one, pltpu.VMEM) for one in sums])
 
 
 def solution(mesh):

time: 32 us -> 29.2 us (0.912)
  local copies, waits for them, and re-layouts: 2.72 us -> 0 us
    unnamed x4 -> x0, local copies, waits for them, and re-layouts: 2.72 us -> none
    pallas_call x1, Pallas kernels: 28.4 us -> 27.4 us  [on_device(): pl.pallas_call(functools.partial(kernel, blocks, groups, reach), out_shap...]
    pallas_call x0 -> x1, Pallas kernels: none -> 0.99 us  [on_device(): pl.pallas_call(leave, out_shape=(jax.ShapeDtypeStruct(ph_in.shape, f32),...]
where the time goes in v2:
time: 29.2 us; the launch traced here: 29 us
  Pallas kernels  28.4 us (97%)
  between operations  0.64 us (2%)
    pallas_call x1, Pallas kernels, on_device(): pl.pallas_call(functools.partial(kernel, blocks, groups, reach), out_shap...  27.4 us
    pallas_call x1, Pallas kernels, on_device(): pl.pallas_call(leave, out_shape=(jax.ShapeDtypeStruct(ph_in.shape, f32),...  0.99 us

profile of v2, /device:TPU:0, one launch (start us, length us, event | category | flops | bytes accessed | tf_op | source)
XLA Modules:
  0.0 29.0 jit_solution(1536101328947977313)
XLA Ops:
  0.6 27.4 %shard_map.68 = (f32[2,4,64,256]{3,2,1,0:T(8,128)S(1)}, f32[2,4,64,256]{3,2,1,0:T(8,128)S(1)}) custom-call(s32[4,256]{1,0:T(4,128)} %shift_ref.1, bf16[1,2,256,256]{3,2,1,0:T(8,128)(2,1)} %masses_ref.1, s32[1,256]{1,0:T(1,128)} %spins_ref.1, f32[2,4,64,256]{3,2,1,0:T(8,128)} %ph_ref.1, f32[2,4,64,256]{3,2,1,0:T(8,128)} %pp_ref.1), custom_call_target="tpu_custom_call" | custom-call | tf_op jit(solution)/shard_map/pallas_call | solution.py:488
  28.0 1.0 %shard_map.69 = (f32[2,4,64,256]{3,2,1,0:T(8,128)}, f32[2,4,64,256]{3,2,1,0:T(8,128)}) custom-call(f32[2,4,64,256]{3,2,1,0:T(8,128)S(1)} %get-tuple-element.4.ph_sum, f32[2,4,64,256]{3,2,1,0:T(8,128)S(1)} %get-tuple-element.5.pp_sum), custom_call_target="tpu_custom_call" | custom-call | tf_op jit(solution)/shard_map/pallas_call | solution.py:514

commit v3 on v2

--- a/solution.py
+++ b/solution.py
@@ -12,6 +12,7 @@
 NK = 16
 COUPLING = 0.5
 VMEM = 67043328
+LANES = 128
 MESH = pl.DeviceIdType.MESH
 NT = (((1,), (1,)), ((), ()))
 
@@ -22,10 +23,6 @@
 
 def base_steps(row, col):
     return ((2 * (row // NK) + 1) * (col // NK) - 2 * (row % NK) * (col % NK)) % (2 * NW)
-
-
-def move_steps(freq, mom, col):
-    return (2 * freq * (col // NK) - 2 * mom * (col % NK)) % (2 * NW)
 
 
 def whole_gather(blocks, groups, reach):
@@ -294,19 +291,17 @@
                 self.relay(offset, step).wait_send()
 
 def kernel(
-    blocks, groups, reach, shift_ref, masses_ref, spins_ref, ph_ref, pp_ref, ph_out, pp_out,
-    held, held_spins, col_table, sh_cols, fl_cols, band, sh_rows, fl_rows,
-    x_ph, x_pp, fixed, recv_sem, send_sem, local_sem,
+    blocks, groups, reach, shift_ref, masses_ref, spins_ref, ph_ref, pp_ref,
+    sums, ph_keep, pp_keep, held, held_spins, steps, band, unit, skew, props, fixed,
+    recv_sem, send_sem, local_sem,
 ):
     group = lax.axis_index("grp")
     block = lax.axis_index("blk")
     order = held.shape[-1]
     walkers = held.shape[1]
-    trans = ph_out.shape[1]
+    trans = sums.shape[0]
     height = order // groups
-    chips = groups // 2
-    chip, core = group // 2, group % 2
-    partner = chip * 2 + (1 - core)
+    lanes = sums.shape[-1]
     f32, bf16 = jnp.float32, jnp.bfloat16
     gather = whole_gather(blocks, groups, reach)
     home = block if gather else 0
@@ -314,8 +309,8 @@
     local = [
         pltpu.make_async_copy(masses_ref, held.at[home], local_sem.at[0]),
         pltpu.make_async_copy(spins_ref, held_spins.at[home], local_sem.at[1]),
-        pltpu.make_async_copy(ph_ref, ph_out, local_sem.at[2]),
-        pltpu.make_async_copy(pp_ref, pp_out, local_sem.at[3]),
+        pltpu.make_async_copy(ph_ref, ph_keep, local_sem.at[2]),
+        pltpu.make_async_copy(pp_ref, pp_keep, local_sem.at[3]),
     ]
     if gather:
         plan = Gather(
@@ -334,87 +329,76 @@
     plan.begin()
 
     norm = 1.0 / math.sqrt(NW * NK)
-    index_col = lax.broadcasted_iota(jnp.int32, (order, 128), 0)
-    lane = lax.broadcasted_iota(jnp.int32, (order, 128), 1)
-    freq = jnp.zeros((order, 128), jnp.int32)
-    mom = jnp.zeros((order, 128), jnp.int32)
-    for t in range(trans):
-        start = shift_ref[t, 0]
-        freq = jnp.where(lane == t, start // NK, freq)
-        mom = jnp.where(lane == t, start % NK, mom)
-    move = angle(move_steps(freq, mom, index_col))
-    move_cos, move_sin = jnp.cos(move), jnp.sin(move)
-
-    def put_cols(ref, t, real, imag):
-        where = (slice(None),) if t is None else (t, slice(None))
-        real, imag = (real * norm).astype(bf16), (imag * norm).astype(bf16)
-        ref[where[:-1] + (slice(0, order), slice(0, order))] = real
-        ref[where[:-1] + (slice(0, order), slice(order, 2 * order))] = -imag
-        ref[where[:-1] + (slice(order, 2 * order), slice(0, order))] = imag
-        ref[where[:-1] + (slice(order, 2 * order), slice(order, 2 * order))] = real
-
-    site = lax.broadcasted_iota(jnp.int32, (order, order), 0)
-    momentum = lax.broadcasted_iota(jnp.int32, (order, order), 1)
-    phase = angle(base_steps(momentum, site))
-    cos, sin = jnp.cos(phase), jnp.sin(phase)
-    put_cols(col_table, None, cos, sin)
-    for t in range(trans):
-        mc, ms = move_cos[:, t : t + 1], move_sin[:, t : t + 1]
-        cc, ss, sc, cs = mc * cos, ms * sin, ms * cos, mc * sin
-        put_cols(sh_cols, t, cc - ss, sc + cs)
-        put_cols(fl_cols, t, cc + ss, sc - cs)
-
-    row = lax.broadcasted_iota(jnp.int32, (height, order), 0) + group * height
-    column = lax.broadcasted_iota(jnp.int32, (height, order), 1)
+    row = lax.broadcasted_iota(jnp.int32, (order, order), 0)
+    column = lax.broadcasted_iota(jnp.int32, (order, order), 1)
     phase = angle(base_steps(row, column))
     cos, sin = jnp.cos(phase), jnp.sin(phase)
-    band[0:height, :] = (cos * norm).astype(bf16)
-    band[height : 2 * height, :] = (sin * norm).astype(bf16)
-    col8 = lax.broadcasted_iota(jnp.int32, (8, order), 1)
-    for t in range(trans):
-        start = shift_ref[t, 0]
-        move = angle(move_steps(start // NK, start % NK, col8))
-        mc, ms = jnp.cos(move)[0:1], jnp.sin(move)[0:1]
-        cc, ss, sc, cs = mc * cos, ms * sin, ms * cos, mc * sin
-        first = 2 * t * height
-        sh_rows[first : first + height, :] = ((cc - ss) * norm).astype(bf16)
-        sh_rows[first + height : first + 2 * height, :] = ((sc + cs) * norm).astype(bf16)
-        fl_rows[first : first + height, :] = ((cc + ss) * norm).astype(bf16)
-        fl_rows[first + height : first + 2 * height, :] = ((sc - cs) * norm).astype(bf16)
+    unit[0], unit[1] = cos, sin
+    steps[0:order] = (cos * norm).astype(bf16)
+    steps[order:] = (sin * norm).astype(bf16)
+    mine = pl.ds(pl.multiple_of(group * height, height), height)
+    band[0:height] = (unit[0, mine] * norm).astype(bf16)
+    band[height:] = (unit[1, mine] * norm).astype(bf16)
+    start = angle(lax.broadcasted_iota(jnp.int32, (8, order), 1) // NK)
+    start_cos, start_sin = jnp.cos(start)[0:1], jnp.sin(start)[0:1]
+    even = ((cos * start_cos + sin * start_sin) * norm).astype(bf16)
+    odd = ((sin * start_cos - cos * start_sin) * norm).astype(bf16)
+    skew[0:order, 0:order] = even
+    skew[0:order, order:] = -odd
+    skew[order:, 0:order] = odd
+    skew[order:, order:] = even
+    sums[...] = jnp.zeros(sums.shape, f32)
 
     def dot(a, b):
         return jnp.dot(a, b, preferred_element_type=f32)
 
-    def absorb(slot):
-        for w in range(walkers):
-            place = pl.ds(pl.multiple_of((slot * walkers + w) * height, height), height)
-            signed = (2 * held_spins[slot, w : w + 1, :] - 1).astype(f32)
-            lefts = []
-            for s in range(2):
-                factor = jnp.exp((COUPLING if s == 0 else -COUPLING) * signed)
-                scaled = (held[slot, w, s].astype(f32) * factor).astype(bf16)
-                moved = dot(sh_rows[...], scaled).astype(bf16)
-                for t in range(trans):
-                    first = 2 * t * height
-                    x_ph[t, s, place, 0:order] = moved[first : first + height]
-                    x_ph[t, s, place, order:] = moved[first + height : first + 2 * height]
-                if s == 1:
-                    moved = dot(fl_rows[...], scaled).astype(bf16)
-                    for t in range(trans):
-                        first = 2 * t * height
-                        x_pp[t, place, 0:order] = moved[first : first + height]
-                        x_pp[t, place, order:] = moved[first + height : first + 2 * height]
-                else:
-                    upper = dot(band[...], scaled).astype(bf16)
-                left = lax.dot_general(band[...], scaled, NT, preferred_element_type=f32)
-                lefts.append(left.astype(bf16))
-            lefts.append(upper)
-            joined = jnp.concatenate(
-                [jnp.concatenate([one[:height], one[height:]], 1) for one in lefts], 0
-            )
-            second = dot(joined, col_table[...])
-            for part in range(3):
-                fixed[part, place, :] = second[part * height : (part + 1) * height]
+    def absorb(slot, w):
+        signed = (2 * held_spins[slot, w : w + 1, :] - 1).astype(f32)
+        for s in range(2):
+            factor = jnp.exp((COUPLING if s == 0 else -COUPLING) * signed)
+            scaled = (held[slot, w, s].astype(f32) * factor).astype(bf16)
+            first = dot(steps[...], scaled)
+            real, imag = first[:order], first[order:]
+            turned = jnp.concatenate(
+                [real * unit[0] + imag * unit[1], imag * unit[0] - real * unit[1]], 1
+            ).astype(bf16)
+            left = lax.dot_general(band[...], scaled, NT, preferred_element_type=f32)
+            real, imag = left[:height], left[height:]
+            mine_cos, mine_sin = unit[0, mine], unit[1, mine]
+            back = jnp.concatenate(
+                [mine_cos * real + mine_sin * imag, mine_cos * imag - mine_sin * real], 1
+            ).astype(bf16)
+            moving = dot(turned, skew[...])
+            kept = dot(back, skew[...])
+            for part in range(2):
+                for half in range(order // lanes):
+                    here = slice(part * order + half * lanes, part * order + (half + 1) * lanes)
+                    fixed[s, part, half] = kept[:, here]
+                    tile = moving[:, here].reshape(NW, NK, lanes)
+                    props[s, part, half, :, 0:NK] = tile
+                    props[s, part, half, :, NK:] = tile
+
+        @pl.loop(0, trans)
+        def _(t):
+            freq, mom = shift_ref[t, 0] // NK, shift_ref[t, 0] % NK
+            ahead, behind = pl.ds(mom, NK), pl.ds(lax.rem(NK - mom, NK), NK)
+            for i in range(height // NK):
+                place = slice(i * NK, (i + 1) * NK)
+                at = group * (height // NK) + i
+                up, down = lax.rem(at + freq, NW), lax.rem(at - freq + NW, NW)
+                for half in range(order // lanes):
+                    real, imag = sums[t, 0, half, place], sums[t, 1, half, place]
+                    for s in range(2):
+                        a, b = fixed[s, 0, half, place], fixed[s, 1, half, place]
+                        c, d = props[s, 0, half, up, ahead], props[s, 1, half, up, ahead]
+                        real = real + (a * c + b * d)
+                        imag = imag + (a * d - b * c)
+                    sums[t, 0, half, place] = real
+                    sums[t, 1, half, place] = imag
+                    a, b = props[0, 0, half, at, 0:NK], props[0, 1, half, at, 0:NK]
+                    c, d = props[1, 0, half, down, behind], props[1, 1, half, down, behind]
+                    sums[t, 2, half, place] += a * c + b * d
+                    sums[t, 3, half, place] += b * c - a * d
 
     @pl.loop(0, reach + 1)
     def _(k):
@@ -424,47 +408,35 @@
             local[1].wait()
 
         plan.turn(k)
-        absorb(plan.slot_at(k))
+        for w in range(walkers):
+            absorb(plan.slot_at(k), w)
 
     local[2].wait()
     local[3].wait()
-    length = (reach + 1) * walkers
-
-    def product(left, right):
-        for v in range(length):
-            part = slice(v * height, (v + 1) * height)
-            a, b = left[part, 0:order], left[part, order:]
-            c, d = right[part, 0:order], right[part, order:]
-            yield a, b, c, d
-
-    @pl.loop(0, trans)
-    def _(t):
-        real, imag = ph_out[0, t], ph_out[1, t]
-        for s in range(2):
-            moved = dot(x_ph[t, s], sh_cols[t])
-            for a, b, c, d in product(fixed[s], moved):
-                real = real + (a * c + b * d)
-                imag = imag + (a * d - b * c)
-        ph_out[0, t] = real
-        ph_out[1, t] = imag
-        real, imag = pp_out[0, t], pp_out[1, t]
-        lowered = dot(x_pp[t], fl_cols[t])
-        for a, b, c, d in product(fixed[2], lowered):
-            real = real + (a * c - b * d)
-            imag = imag + (a * d + b * c)
-        pp_out[0, t] = real
-        pp_out[1, t] = imag
-
     plan.drain()
 
 
-def leave(ph_sum, pp_sum, ph_out, pp_out, sem):
-    copies = [
-        pltpu.make_async_copy(ph_sum, ph_out, sem.at[0]),
-        pltpu.make_async_copy(pp_sum, pp_out, sem.at[1]),
-    ]
-    for copy in copies:
-        copy.start()
+def leave(groups, sums, ph_keep, pp_keep, ph_out, pp_out, ph_new, pp_new, sem):
+    trans, _, _, height, lanes = sums.shape
+    group = lax.axis_index("grp")
+    row = lax.broadcasted_iota(jnp.int32, (height, lanes), 0)
+    lane = lax.broadcasted_iota(jnp.int32, (height, lanes), 1)
+    freq = (lane // NK - group * (height // NK) - row // NK + 2 * NW) % NW
+    mom = (lane % NK - row % NK + NK) % NK
+    source = freq * NK + mom
+    index, upper = source % lanes, source >= lanes
+    copies = []
+    for t in range(trans):
+        for keep, new, first in ((ph_keep, ph_new, 0), (pp_keep, pp_new, 2)):
+            for part in range(2):
+                low, high = [
+                    jnp.take_along_axis(sums[t, first + part, half], index, 1) for half in range(2)
+                ]
+                new[part, t, :, 0:lanes] = keep[part, t, :, 0:lanes] + jnp.where(upper, high, low)
+                new[part, t, :, lanes:] = keep[part, t, :, lanes:] + jnp.where(upper, low, high)
+        for i, (new, out) in enumerate(((ph_new, ph_out), (pp_new, pp_out))):
+            copies.append(pltpu.make_async_copy(new.at[:, t], out.at[:, t], sem.at[t, i]))
+            copies[-1].start()
     for copy in copies:
         copy.wait()
 
@@ -479,6 +451,7 @@
     height = order // groups
     chips = groups // 2
     f32, bf16 = jnp.float32, jnp.bfloat16
+    sums_shape = (trans, 4, order // LANES, height, LANES)
     dma = pltpu.SemaphoreType.DMA
     anywhere = pl.BlockSpec(memory_space=pl.ANY)
     if whole_gather(blocks, groups, reach):
@@ -487,39 +460,45 @@
         recv_shape, send_shape = (visits, groups + 1), (visits, 3 + 2 * (chips - 1))
     sums = pl.pallas_call(
         functools.partial(kernel, blocks, groups, reach),
-        out_shape=(pltpu.VMEM(ph_in.shape, f32), pltpu.VMEM(pp_in.shape, f32)),
+        out_shape=(
+            pltpu.VMEM(sums_shape, f32),
+            pltpu.VMEM(ph_in.shape, f32),
+            pltpu.VMEM(pp_in.shape, f32),
+        ),
         in_specs=[pl.BlockSpec(memory_space=pltpu.SMEM)]
         + [pl.BlockSpec(memory_space=pltpu.HBM)] * 4,
-        out_specs=(pl.BlockSpec(memory_space=pltpu.VMEM),) * 2,
+        out_specs=(pl.BlockSpec(memory_space=pltpu.VMEM),) * 3,
         scratch_shapes=[
             pltpu.VMEM((visits, walkers, 2, order, order), bf16),
             pltpu.VMEM((visits, walkers, order), jnp.int32),
+            pltpu.VMEM((2 * order, order), bf16),
+            pltpu.VMEM((2 * height, order), bf16),
+            pltpu.VMEM((2, order, order), f32),
             pltpu.VMEM((2 * order, 2 * order), bf16),
-            pltpu.VMEM((trans, 2 * order, 2 * order), bf16),
-            pltpu.VMEM((trans, 2 * order, 2 * order), bf16),
-            pltpu.VMEM((2 * height, order), bf16),
-            pltpu.VMEM((trans * 2 * height, order), bf16),
-            pltpu.VMEM((trans * 2 * height, order), bf16),
-            pltpu.VMEM((trans, 2, visits * walkers * height, 2 * order), bf16),
-            pltpu.VMEM((trans, visits * walkers * height, 2 * order), bf16),
-            pltpu.VMEM((3, visits * walkers * height, 2 * order), f32),
+            pltpu.VMEM((2, 2, order // LANES, NW, 2 * NK, LANES), f32),
+            pltpu.VMEM((2, 2, order // LANES, height, LANES), f32),
             dma(recv_shape),
             dma(send_shape),
             dma((4,)),
         ],
         compiler_params=pltpu.CompilerParams(
-            collective_id=0, has_side_effects=True, vmem_limit_bytes=VMEM - 4 * (ph_in.size + pp_in.size) - 65536
+            collective_id=0, has_side_effects=True, vmem_limit_bytes=VMEM - 8 * (ph_in.size + pp_in.size) - 65536
         ),
     )(shift_table, masses, spins, ph_in, pp_in)
     return pl.pallas_call(
-        leave,
+        functools.partial(leave, groups),
         out_shape=(
             jax.ShapeDtypeStruct(ph_in.shape, f32),
             jax.ShapeDtypeStruct(pp_in.shape, f32),
         ),
-        in_specs=[pl.BlockSpec(memory_space=pltpu.VMEM)] * 2,
+        in_specs=[pl.BlockSpec(memory_space=pltpu.VMEM)] * 3,
         out_specs=(anywhere,) * 2,
-        scratch_shapes=[dma((2,))],
+        scratch_shapes=[
+            pltpu.VMEM(ph_in.shape, f32),
+            pltpu.VMEM(pp_in.shape, f32),
+            dma((trans, 2)),
+        ],
+        compiler_params=pltpu.CompilerParams(vmem_limit_bytes=16 * 1024 * 1024),
     )(*[pltpu.with_memory_space_constraint(one, pltpu.VMEM) for one in sums])
 
 

time: 29.2 us -> 29.6 us (1.014); the launches traced: 29 us -> 29 us
    pallas_call x1, Pallas kernels: 27.4 us -> 26.8 us  [on_device(): pl.pallas_call(functools.partial(kernel, blocks, groups, reach), out_shap...]
    pallas_call x1, Pallas kernels: 0.99 us -> 1.54 us  [on_device(): pl.pallas_call(functools.partial(leave, groups), out_shape=(jax.ShapeDtyp...]
where the time goes in v3:
time: 29.6 us; the launch traced here: 29 us
  Pallas kernels  28.3 us (96%)
  between operations  0.64 us (2%)
    pallas_call x1, Pallas kernels, on_device(): pl.pallas_call(functools.partial(kernel, blocks, groups, reach), out_shap...  26.8 us
    pallas_call x1, Pallas kernels, on_device(): pl.pallas_call(functools.partial(leave, groups), out_shape=(jax.ShapeDtyp...  1.54 us

profile of v3, /device:TPU:0, one launch (start us, length us, event | category | flops | bytes accessed | tf_op | source)
XLA Modules:
  0.0 29.0 jit_solution(14695381604563182901)
XLA Ops:
  0.6 26.8 %shard_map.68 = (f32[4,4,2,64,128]{4,3,2,1,0:T(8,128)S(1)}, f32[2,4,64,256]{3,2,1,0:T(8,128)S(1)}, f32[2,4,64,256]{3,2,1,0:T(8,128)S(1)}) custom-call(s32[4,256]{1,0:T(4,128)} %shift_ref.1, bf16[1,2,256,256]{3,2,1,0:T(8,128)(2,1)} %masses_ref.1, s32[1,256]{1,0:T(1,128)} %spins_ref.1, f32[2,4,64,256]{3,2,1,0:T(8,128)} %ph_ref.1, f32[2,4,64,256]{3,2,1,0:T(8,128)} %pp_ref.1), custom_call_target="tpu_custom_call" | custom-call | tf_op jit(solution)/shard_map/pallas_call | solution.py:461
  27.4 1.5 %shard_map.69 = (f32[2,4,64,256]{3,2,1,0:T(8,128)}, f32[2,4,64,256]{3,2,1,0:T(8,128)}) custom-call(f32[4,4,2,64,128]{4,3,2,1,0:T(8,128)S(1)} %get-tuple-element.5.sums, f32[2,4,64,256]{3,2,1,0:T(8,128)S(1)} %get-tuple-element.6.ph_keep, f32[2,4,64,256]{3,2,1,0:T(8,128)S(1)} %get-tuple-element.7.pp_keep), custom_call_target="tpu_custom_call" | custom-call | tf_op jit(solution)/shard_map/pallas_call | solution.py:488

commit v4 on v3

--- a/solution.py
+++ b/solution.py
@@ -13,16 +13,13 @@
 COUPLING = 0.5
 VMEM = 67043328
 LANES = 128
+ROWS = 8
 MESH = pl.DeviceIdType.MESH
 NT = (((1,), (1,)), ((), ()))
 
 
 def angle(steps):
     return steps.astype(jnp.float32) * (math.pi / NW)
-
-
-def base_steps(row, col):
-    return ((2 * (row // NK) + 1) * (col // NK) - 2 * (row % NK) * (col % NK)) % (2 * NW)
 
 
 def whole_gather(blocks, groups, reach):
@@ -45,7 +42,7 @@
 
 
 class Gather:
-    TURNS = ("", "O0 O1 H0 I0", "H1 h0 F0", "F1 i0 I1", "h1 f0", "f1 i1", "", "")
+    TURNS = ("", "O0 O1 H0 I0", "H1 h0 F0", "F1 i0 I1", "", "h1 f0 f1 i1", "", "")
     SLOTS = "SOHFIhfi"
 
     def __init__(self, group, block, order, walkers, masses, spins, held, held_spins, recv, sends):
@@ -329,76 +326,114 @@
     plan.begin()
 
     norm = 1.0 / math.sqrt(NW * NK)
-    row = lax.broadcasted_iota(jnp.int32, (order, order), 0)
-    column = lax.broadcasted_iota(jnp.int32, (order, order), 1)
-    phase = angle(base_steps(row, column))
-    cos, sin = jnp.cos(phase), jnp.sin(phase)
-    unit[0], unit[1] = cos, sin
-    steps[0:order] = (cos * norm).astype(bf16)
-    steps[order:] = (sin * norm).astype(bf16)
+    row = lax.broadcasted_iota(jnp.int32, (NW, order), 0)
+    column = lax.broadcasted_iota(jnp.int32, (NW, order), 1)
+    slices, sites = column // NK, column % NK
+
+    def circle(numerator):
+        turn = angle(numerator % (2 * NW))
+        return jnp.cos(turn), jnp.sin(turn)
+
+    site_cos, site_sin = circle(2 * NW * NK - 2 * row * sites)
+    odd_cos, odd_sin = circle((2 * row + 1) * slices)
+    even_cos, even_sin = circle(2 * row * slices)
+    for i in range(NW):
+        here = slice(i * NK, (i + 1) * NK)
+        c, d = odd_cos[i : i + 1], odd_sin[i : i + 1]
+        cos, sin = c * site_cos - d * site_sin, d * site_cos + c * site_sin
+        unit[0, here], unit[1, here] = cos, sin
+        if i < NW // 2:
+            steps[here] = (cos * norm).astype(bf16)
+            steps[order // 2 + i * NK : order // 2 + (i + 1) * NK] = (sin * norm).astype(bf16)
+        c, d = even_cos[i : i + 1], even_sin[i : i + 1]
+        skew[here, 0:order] = ((c * site_cos - d * site_sin) * norm).astype(bf16)
+        skew[here, order:] = ((d * site_cos + c * site_sin) * norm).astype(bf16)
     mine = pl.ds(pl.multiple_of(group * height, height), height)
     band[0:height] = (unit[0, mine] * norm).astype(bf16)
     band[height:] = (unit[1, mine] * norm).astype(bf16)
-    start = angle(lax.broadcasted_iota(jnp.int32, (8, order), 1) // NK)
-    start_cos, start_sin = jnp.cos(start)[0:1], jnp.sin(start)[0:1]
-    even = ((cos * start_cos + sin * start_sin) * norm).astype(bf16)
-    odd = ((sin * start_cos - cos * start_sin) * norm).astype(bf16)
-    skew[0:order, 0:order] = even
-    skew[0:order, order:] = -odd
-    skew[order:, 0:order] = odd
-    skew[order:, order:] = even
     sums[...] = jnp.zeros(sums.shape, f32)
 
     def dot(a, b):
         return jnp.dot(a, b, preferred_element_type=f32)
 
+    middle = order // 2
+    flip = ROWS - 1 - lax.broadcasted_iota(jnp.int32, (ROWS, lanes), 0)
+
+    def put(s, part, half, lower, upper):
+        for i in range(NW // 2):
+            tiles = [lower[i * NK + r : i * NK + r + ROWS] for r in range(0, NK, ROWS)]
+            for r, tile in enumerate(tiles + tiles[:1]):
+                props[s, part, half, i, r * ROWS : (r + 1) * ROWS] = tile
+            tiles = [upper[i * NK + r : i * NK + r + ROWS] for r in range(0, NK, ROWS)]
+            tiles = [jnp.take_along_axis(tile, flip, 0) for tile in tiles[::-1]]
+            for r, tile in enumerate(tiles + tiles[:1]):
+                props[s, part, half, NW - 1 - i, r * ROWS : (r + 1) * ROWS] = tile
+
+    def from_row(freq, mom):
+        mirrored = (freq >= NW // 2).astype(jnp.int32)
+        return pl.ds(lax.rem(mom - mirrored + NK, NK), ROWS)
+
     def absorb(slot, w):
         signed = (2 * held_spins[slot, w : w + 1, :] - 1).astype(f32)
+        turned, back = [], []
         for s in range(2):
             factor = jnp.exp((COUPLING if s == 0 else -COUPLING) * signed)
             scaled = (held[slot, w, s].astype(f32) * factor).astype(bf16)
-            first = dot(steps[...], scaled)
-            real, imag = first[:order], first[order:]
-            turned = jnp.concatenate(
-                [real * unit[0] + imag * unit[1], imag * unit[0] - real * unit[1]], 1
-            ).astype(bf16)
             left = lax.dot_general(band[...], scaled, NT, preferred_element_type=f32)
             real, imag = left[:height], left[height:]
-            mine_cos, mine_sin = unit[0, mine], unit[1, mine]
-            back = jnp.concatenate(
-                [mine_cos * real + mine_sin * imag, mine_cos * imag - mine_sin * real], 1
-            ).astype(bf16)
-            moving = dot(turned, skew[...])
-            kept = dot(back, skew[...])
-            for part in range(2):
-                for half in range(order // lanes):
-                    here = slice(part * order + half * lanes, part * order + (half + 1) * lanes)
-                    fixed[s, part, half] = kept[:, here]
-                    tile = moving[:, here].reshape(NW, NK, lanes)
-                    props[s, part, half, :, 0:NK] = tile
-                    props[s, part, half, :, NK:] = tile
+            cos, sin = unit[0, mine], unit[1, mine]
+            back += [
+                (cos * real + sin * imag).astype(bf16),
+                (sin * real - cos * imag).astype(bf16),
+            ]
+            first = dot(steps[...], scaled)
+            real, imag = first[:middle], first[middle:]
+            cos, sin = unit[0, 0:middle], unit[1, 0:middle]
+            turned += [
+                (real * cos + imag * sin).astype(bf16),
+                (imag * cos - real * sin).astype(bf16),
+            ]
+        moving = dot(jnp.concatenate(turned + back, 0), skew[...])
+        for s in range(2):
+            for half in range(order // lanes):
+                even = slice(half * lanes, (half + 1) * lanes)
+                odd = slice(order + half * lanes, order + (half + 1) * lanes)
+                real = moving[s * order : s * order + middle]
+                imag = moving[s * order + middle : (s + 1) * order]
+                put(s, 0, half, real[:, even] + imag[:, odd], real[:, even] - imag[:, odd])
+                put(s, 1, half, imag[:, even] - real[:, odd], -imag[:, even] - real[:, odd])
+                first = 2 * order + 2 * s * height
+                real = moving[first : first + height]
+                imag = moving[first + height : first + 2 * height]
+                fixed[s, 0, half] = real[:, even] - imag[:, odd]
+                fixed[s, 1, half] = -real[:, odd] - imag[:, even]
 
         @pl.loop(0, trans)
         def _(t):
             freq, mom = shift_ref[t, 0] // NK, shift_ref[t, 0] % NK
-            ahead, behind = pl.ds(mom, NK), pl.ds(lax.rem(NK - mom, NK), NK)
             for i in range(height // NK):
-                place = slice(i * NK, (i + 1) * NK)
                 at = group * (height // NK) + i
                 up, down = lax.rem(at + freq, NW), lax.rem(at - freq + NW, NW)
-                for half in range(order // lanes):
-                    real, imag = sums[t, 0, half, place], sums[t, 1, half, place]
-                    for s in range(2):
-                        a, b = fixed[s, 0, half, place], fixed[s, 1, half, place]
-                        c, d = props[s, 0, half, up, ahead], props[s, 1, half, up, ahead]
-                        real = real + (a * c + b * d)
-                        imag = imag + (a * d - b * c)
-                    sums[t, 0, half, place] = real
-                    sums[t, 1, half, place] = imag
-                    a, b = props[0, 0, half, at, 0:NK], props[0, 1, half, at, 0:NK]
-                    c, d = props[1, 0, half, down, behind], props[1, 1, half, down, behind]
-                    sums[t, 2, half, place] += a * c + b * d
-                    sums[t, 3, half, place] += b * c - a * d
+                for piece in range(NK // ROWS):
+                    rows = i * NK + piece * ROWS
+                    place = slice(rows, rows + ROWS)
+                    offset = piece * ROWS
+                    ahead = from_row(up, mom + offset)
+                    behind = from_row(down, NK - mom + offset)
+                    own = from_row(at, offset)
+                    for half in range(order // lanes):
+                        real, imag = sums[t, 0, half, place], sums[t, 1, half, place]
+                        for s in range(2):
+                            a, b = fixed[s, 0, half, place], fixed[s, 1, half, place]
+                            c, d = props[s, 0, half, up, ahead], props[s, 1, half, up, ahead]
+                            real = real + (a * c + b * d)
+                            imag = imag + (a * d - b * c)
+                        sums[t, 0, half, place] = real
+                        sums[t, 1, half, place] = imag
+                        a, b = props[0, 0, half, at, own], props[0, 1, half, at, own]
+                        c, d = props[1, 0, half, down, behind], props[1, 1, half, down, behind]
+                        sums[t, 2, half, place] += a * c + b * d
+                        sums[t, 3, half, place] += b * c - a * d
 
     @pl.loop(0, reach + 1)
     def _(k):
@@ -471,11 +506,11 @@
         scratch_shapes=[
             pltpu.VMEM((visits, walkers, 2, order, order), bf16),
             pltpu.VMEM((visits, walkers, order), jnp.int32),
-            pltpu.VMEM((2 * order, order), bf16),
+            pltpu.VMEM((order, order), bf16),
             pltpu.VMEM((2 * height, order), bf16),
             pltpu.VMEM((2, order, order), f32),
-            pltpu.VMEM((2 * order, 2 * order), bf16),
-            pltpu.VMEM((2, 2, order // LANES, NW, 2 * NK, LANES), f32),
+            pltpu.VMEM((order, 2 * order), bf16),
+            pltpu.VMEM((2, 2, order // LANES, NW, NK + ROWS, LANES), f32),
             pltpu.VMEM((2, 2, order // LANES, height, LANES), f32),
             dma(recv_shape),
             dma(send_shape),

time: 29.6 us -> 28.5 us (0.963); the launches traced: 29 us -> 28.3 us
  Pallas kernels: 28.3 us -> 27.6 us
    pallas_call x1, Pallas kernels: 26.8 us -> 26.1 us  [on_device(): pl.pallas_call(functools.partial(kernel, blocks, groups, reach), out_shap...]
where the time goes in v4:
time: 28.5 us; the launch traced here: 28.3 us
  Pallas kernels  27.6 us (97%)
  between operations  0.64 us (2%)
    pallas_call x1, Pallas kernels, on_device(): pl.pallas_call(functools.partial(kernel, blocks, groups, reach), out_shap...  26.1 us
    pallas_call x1, Pallas kernels, on_device(): pl.pallas_call(functools.partial(leave, groups), out_shape=(jax.ShapeDtyp...  1.54 us

profile of v4, /device:TPU:0, one launch (start us, length us, event | category | flops | bytes accessed | tf_op | source)
XLA Modules:
  0.0 28.3 jit_solution(6504052965527037691)
XLA Ops:
  0.6 26.1 %shard_map.68 = (f32[4,4,2,64,128]{4,3,2,1,0:T(8,128)S(1)}, f32[2,4,64,256]{3,2,1,0:T(8,128)S(1)}, f32[2,4,64,256]{3,2,1,0:T(8,128)S(1)}) custom-call(s32[4,256]{1,0:T(4,128)} %shift_ref.1, bf16[1,2,256,256]{3,2,1,0:T(8,128)(2,1)} %masses_ref.1, s32[1,256]{1,0:T(1,128)} %spins_ref.1, f32[2,4,64,256]{3,2,1,0:T(8,128)} %ph_ref.1, f32[2,4,64,256]{3,2,1,0:T(8,128)} %pp_ref.1), custom_call_target="tpu_custom_call" | custom-call | tf_op jit(solution)/shard_map/pallas_call | solution.py:496
  26.7 1.5 %shard_map.69 = (f32[2,4,64,256]{3,2,1,0:T(8,128)}, f32[2,4,64,256]{3,2,1,0:T(8,128)}) custom-call(f32[4,4,2,64,128]{4,3,2,1,0:T(8,128)S(1)} %get-tuple-element.5.sums, f32[2,4,64,256]{3,2,1,0:T(8,128)S(1)} %get-tuple-element.6.ph_keep, f32[2,4,64,256]{3,2,1,0:T(8,128)S(1)} %get-tuple-element.7.pp_keep), custom_call_target="tpu_custom_call" | custom-call | tf_op jit(solution)/shard_map/pallas_call | solution.py:523

commit v5 on v4

--- a/solution.py
+++ b/solution.py
@@ -42,8 +42,8 @@
 
 
 class Gather:
-    TURNS = ("", "O0 O1 H0 I0", "H1 h0 F0", "F1 i0 I1", "", "h1 f0 f1 i1", "", "")
-    SLOTS = "SOHFIhfi"
+    TURNS = ('', 'H0 O0 O1 I0', 'H1 h0 F0', 'F1 i0 I1', 'h1', 'f0 f1 i1', '', '')
+    SLOTS = 'SOHIFhfi'
 
     def __init__(self, group, block, order, walkers, masses, spins, held, held_spins, recv, sends):
         self.chip, self.core = group // 2, group % 2

time: 28.5 us -> 25.6 us (0.90)
  Pallas kernels: 27.6 us -> 24.8 us
    pallas_call x1, Pallas kernels: 26.1 us -> 23.3 us  [on_device(): pl.pallas_call(functools.partial(kernel, blocks, groups, reach), out_shap...]
where the time goes in v5:
time: 25.6 us; the launch traced here: 25.4 us
  Pallas kernels  24.8 us (97%)
  between operations  0.64 us (2%)
    pallas_call x1, Pallas kernels, on_device(): pl.pallas_call(functools.partial(kernel, blocks, groups, reach), out_shap...  23.3 us
    pallas_call x1, Pallas kernels, on_device(): pl.pallas_call(functools.partial(leave, groups), out_shape=(jax.ShapeDtyp...  1.54 us

profile of v5, /device:TPU:0, one launch (start us, length us, event | category | flops | bytes accessed | tf_op | source)
XLA Modules:
  0.0 25.4 jit_solution(394382468232117497)
XLA Ops:
  0.6 23.3 %shard_map.68 = (f32[4,4,2,64,128]{4,3,2,1,0:T(8,128)S(1)}, f32[2,4,64,256]{3,2,1,0:T(8,128)S(1)}, f32[2,4,64,256]{3,2,1,0:T(8,128)S(1)}) custom-call(s32[4,256]{1,0:T(4,128)} %shift_ref.1, bf16[1,2,256,256]{3,2,1,0:T(8,128)(2,1)} %masses_ref.1, s32[1,256]{1,0:T(1,128)} %spins_ref.1, f32[2,4,64,256]{3,2,1,0:T(8,128)} %ph_ref.1, f32[2,4,64,256]{3,2,1,0:T(8,128)} %pp_ref.1), custom_call_target="tpu_custom_call" | custom-call | tf_op jit(solution)/shard_map/pallas_call | solution.py:496
  23.9 1.5 %shard_map.69 = (f32[2,4,64,256]{3,2,1,0:T(8,128)}, f32[2,4,64,256]{3,2,1,0:T(8,128)}) custom-call(f32[4,4,2,64,128]{4,3,2,1,0:T(8,128)S(1)} %get-tuple-element.5.sums, f32[2,4,64,256]{3,2,1,0:T(8,128)S(1)} %get-tuple-element.6.ph_keep, f32[2,4,64,256]{3,2,1,0:T(8,128)S(1)} %get-tuple-element.7.pp_keep), custom_call_target="tpu_custom_call" | custom-call | tf_op jit(solution)/shard_map/pallas_call | solution.py:523

commit v6 on v5

--- a/solution.py
+++ b/solution.py
@@ -14,6 +14,8 @@
 VMEM = 67043328
 LANES = 128
 ROWS = 8
+HALF_BITS = 3
+BITS = 4
 MESH = pl.DeviceIdType.MESH
 NT = (((1,), (1,)), ((), ()))
 
@@ -288,9 +290,9 @@
                 self.relay(offset, step).wait_send()
 
 def kernel(
-    blocks, groups, reach, shift_ref, masses_ref, spins_ref, ph_ref, pp_ref,
+    blocks, groups, reach, table_ref, masses_ref, spins_ref, ph_ref, pp_ref,
     sums, ph_keep, pp_keep, held, held_spins, steps, band, unit, skew, props, fixed,
-    recv_sem, send_sem, local_sem,
+    shift_ref, recv_sem, send_sem, local_sem,
 ):
     group = lax.axis_index("grp")
     block = lax.axis_index("blk")
@@ -308,6 +310,7 @@
         pltpu.make_async_copy(spins_ref, held_spins.at[home], local_sem.at[1]),
         pltpu.make_async_copy(ph_ref, ph_keep, local_sem.at[2]),
         pltpu.make_async_copy(pp_ref, pp_keep, local_sem.at[3]),
+        pltpu.make_async_copy(table_ref, shift_ref, local_sem.at[4]),
     ]
     if gather:
         plan = Gather(
@@ -370,8 +373,8 @@
                 props[s, part, half, NW - 1 - i, r * ROWS : (r + 1) * ROWS] = tile
 
     def from_row(freq, mom):
-        mirrored = (freq >= NW // 2).astype(jnp.int32)
-        return pl.ds(lax.rem(mom - mirrored + NK, NK), ROWS)
+        mirrored = lax.shift_right_logical(freq, HALF_BITS)
+        return pl.ds((mom - mirrored + NK) & (NK - 1), ROWS)
 
     def absorb(slot, w):
         signed = (2 * held_spins[slot, w : w + 1, :] - 1).astype(f32)
@@ -410,10 +413,11 @@
 
         @pl.loop(0, trans)
         def _(t):
-            freq, mom = shift_ref[t, 0] // NK, shift_ref[t, 0] % NK
+            start = shift_ref[t, 0]
+            freq, mom = lax.shift_right_logical(start, BITS), start & (NK - 1)
             for i in range(height // NK):
                 at = group * (height // NK) + i
-                up, down = lax.rem(at + freq, NW), lax.rem(at - freq + NW, NW)
+                up, down = (at + freq) & (NW - 1), (at - freq + NW) & (NW - 1)
                 for piece in range(NK // ROWS):
                     rows = i * NK + piece * ROWS
                     place = slice(rows, rows + ROWS)
@@ -441,6 +445,7 @@
         def _():
             local[0].wait()
             local[1].wait()
+            local[4].wait()
 
         plan.turn(k)
         for w in range(walkers):
@@ -500,8 +505,7 @@
             pltpu.VMEM(ph_in.shape, f32),
             pltpu.VMEM(pp_in.shape, f32),
         ),
-        in_specs=[pl.BlockSpec(memory_space=pltpu.SMEM)]
-        + [pl.BlockSpec(memory_space=pltpu.HBM)] * 4,
+        in_specs=[pl.BlockSpec(memory_space=pltpu.HBM)] * 5,
         out_specs=(pl.BlockSpec(memory_space=pltpu.VMEM),) * 3,
         scratch_shapes=[
             pltpu.VMEM((visits, walkers, 2, order, order), bf16),
@@ -512,9 +516,10 @@
             pltpu.VMEM((order, 2 * order), bf16),
             pltpu.VMEM((2, 2, order // LANES, NW, NK + ROWS, LANES), f32),
             pltpu.VMEM((2, 2, order // LANES, height, LANES), f32),
+            pltpu.SMEM(shift_table.shape, jnp.int32),
             dma(recv_shape),
             dma(send_shape),
-            dma((4,)),
+            dma((5,)),
         ],
         compiler_params=pltpu.CompilerParams(
             collective_id=0, has_side_effects=True, vmem_limit_bytes=VMEM - 8 * (ph_in.size + pp_in.size) - 65536

time: 25.6 us -> 24.7 us (0.965)
  Pallas kernels: 24.8 us -> 23.9 us
    pallas_call x1, Pallas kernels: 23.3 us -> 22.3 us  [on_device(): pl.pallas_call(functools.partial(kernel, blocks, groups, reach), out_shap...]
where the time goes in v6:
time: 24.7 us; the launch traced here: 24.5 us
  Pallas kernels  23.9 us (97%)
  between operations  0.64 us (3%)
    pallas_call x1, Pallas kernels, on_device(): pl.pallas_call(functools.partial(kernel, blocks, groups, reach), out_shap...  22.3 us
    pallas_call x1, Pallas kernels, on_device(): pl.pallas_call(functools.partial(leave, groups), out_shape=(jax.ShapeDtyp...  1.54 us

profile of v6, /device:TPU:0, one launch (start us, length us, event | category | flops | bytes accessed | tf_op | source)
XLA Modules:
  0.0 24.5 jit_solution(12601499141062089796)
XLA Ops:
  0.6 22.3 %shard_map.68 = (f32[4,4,2,64,128]{4,3,2,1,0:T(8,128)S(1)}, f32[2,4,64,256]{3,2,1,0:T(8,128)S(1)}, f32[2,4,64,256]{3,2,1,0:T(8,128)S(1)}) custom-call(s32[4,256]{1,0:T(4,128)} %table_ref.1, bf16[1,2,256,256]{3,2,1,0:T(8,128)(2,1)} %masses_ref.1, s32[1,256]{1,0:T(1,128)} %spins_ref.1, f32[2,4,64,256]{3,2,1,0:T(8,128)} %ph_ref.1, f32[2,4,64,256]{3,2,1,0:T(8,128)} %pp_ref.1), custom_call_target="tpu_custom_call" | custom-call | tf_op jit(solution)/shard_map/pallas_call | solution.py:501
  23.0 1.5 %shard_map.69 = (f32[2,4,64,256]{3,2,1,0:T(8,128)}, f32[2,4,64,256]{3,2,1,0:T(8,128)}) custom-call(f32[4,4,2,64,128]{4,3,2,1,0:T(8,128)S(1)} %get-tuple-element.5.sums, f32[2,4,64,256]{3,2,1,0:T(8,128)S(1)} %get-tuple-element.6.ph_keep, f32[2,4,64,256]{3,2,1,0:T(8,128)S(1)} %get-tuple-element.7.pp_keep), custom_call_target="tpu_custom_call" | custom-call | tf_op jit(solution)/shard_map/pallas_call | solution.py:528

commit v7 on v6

--- a/solution.py
+++ b/solution.py
@@ -44,7 +44,7 @@
 
 
 class Gather:
-    TURNS = ('', 'H0 O0 O1 I0', 'H1 h0 F0', 'F1 i0 I1', 'h1', 'f0 f1 i1', '', '')
+    TURNS = ('', 'H0 O0 I0 O1', 'H1 h0 F0', 'F1 i0 I1', 'h1 f0', 'f1 i1', '', '')
     SLOTS = 'SOHIFhfi'
 
     def __init__(self, group, block, order, walkers, masses, spins, held, held_spins, recv, sends):
@@ -346,31 +346,33 @@
         cos, sin = c * site_cos - d * site_sin, d * site_cos + c * site_sin
         unit[0, here], unit[1, here] = cos, sin
         if i < NW // 2:
-            steps[here] = (cos * norm).astype(bf16)
-            steps[order // 2 + i * NK : order // 2 + (i + 1) * NK] = (sin * norm).astype(bf16)
+            steps[2 * i * NK : (2 * i + 1) * NK] = (cos * norm).astype(bf16)
+            steps[(2 * i + 1) * NK : (2 * i + 2) * NK] = (sin * norm).astype(bf16)
         c, d = even_cos[i : i + 1], even_sin[i : i + 1]
-        skew[here, 0:order] = ((c * site_cos - d * site_sin) * norm).astype(bf16)
-        skew[here, order:] = ((d * site_cos + c * site_sin) * norm).astype(bf16)
-    mine = pl.ds(pl.multiple_of(group * height, height), height)
-    band[0:height] = (unit[0, mine] * norm).astype(bf16)
-    band[height:] = (unit[1, mine] * norm).astype(bf16)
+        cos, sin = c * site_cos - d * site_sin, d * site_cos + c * site_sin
+        for half in range(order // lanes):
+            part = slice(half * lanes, (half + 1) * lanes)
+            skew[half, here, 0:lanes] = (cos[:, part] * norm).astype(bf16)
+            skew[half, here, lanes:] = (sin[:, part] * norm).astype(bf16)
+    for i in range(height // NK):
+        near = pl.ds(pl.multiple_of(group * height + i * NK, NK), NK)
+        band[2 * i * NK : (2 * i + 1) * NK] = (unit[0, near] * norm).astype(bf16)
+        band[(2 * i + 1) * NK : (2 * i + 2) * NK] = (unit[1, near] * norm).astype(bf16)
     sums[...] = jnp.zeros(sums.shape, f32)
 
     def dot(a, b):
         return jnp.dot(a, b, preferred_element_type=f32)
 
-    middle = order // 2
     flip = ROWS - 1 - lax.broadcasted_iota(jnp.int32, (ROWS, lanes), 0)
 
-    def put(s, part, half, lower, upper):
-        for i in range(NW // 2):
-            tiles = [lower[i * NK + r : i * NK + r + ROWS] for r in range(0, NK, ROWS)]
-            for r, tile in enumerate(tiles + tiles[:1]):
-                props[s, part, half, i, r * ROWS : (r + 1) * ROWS] = tile
-            tiles = [upper[i * NK + r : i * NK + r + ROWS] for r in range(0, NK, ROWS)]
-            tiles = [jnp.take_along_axis(tile, flip, 0) for tile in tiles[::-1]]
-            for r, tile in enumerate(tiles + tiles[:1]):
-                props[s, part, half, NW - 1 - i, r * ROWS : (r + 1) * ROWS] = tile
+    def put(s, part, half, i, lower, upper):
+        tiles = [lower[r : r + ROWS] for r in range(0, NK, ROWS)]
+        for r, tile in enumerate(tiles + tiles[:1]):
+            props[s, part, half, i, r * ROWS : (r + 1) * ROWS] = tile
+        tiles = [upper[r : r + ROWS] for r in range(0, NK, ROWS)]
+        tiles = [jnp.take_along_axis(tile, flip, 0) for tile in tiles[::-1]]
+        for r, tile in enumerate(tiles + tiles[:1]):
+            props[s, part, half, NW - 1 - i, r * ROWS : (r + 1) * ROWS] = tile
 
     def from_row(freq, mom):
         mirrored = lax.shift_right_logical(freq, HALF_BITS)
@@ -378,38 +380,44 @@
 
     def absorb(slot, w):
         signed = (2 * held_spins[slot, w : w + 1, :] - 1).astype(f32)
-        turned, back = [], []
+        turned = []
         for s in range(2):
             factor = jnp.exp((COUPLING if s == 0 else -COUPLING) * signed)
             scaled = (held[slot, w, s].astype(f32) * factor).astype(bf16)
+            first = dot(steps[...], scaled)
+            for i in range(NW // 2):
+                real, imag = first[2 * i * NK : (2 * i + 1) * NK], first[(2 * i + 1) * NK : (2 * i + 2) * NK]
+                cos, sin = unit[0, i * NK : (i + 1) * NK], unit[1, i * NK : (i + 1) * NK]
+                turned += [
+                    (real * cos + imag * sin).astype(bf16),
+                    (imag * cos - real * sin).astype(bf16),
+                ]
             left = lax.dot_general(band[...], scaled, NT, preferred_element_type=f32)
-            real, imag = left[:height], left[height:]
-            cos, sin = unit[0, mine], unit[1, mine]
-            back += [
-                (cos * real + sin * imag).astype(bf16),
-                (sin * real - cos * imag).astype(bf16),
-            ]
-            first = dot(steps[...], scaled)
-            real, imag = first[:middle], first[middle:]
-            cos, sin = unit[0, 0:middle], unit[1, 0:middle]
-            turned += [
-                (real * cos + imag * sin).astype(bf16),
-                (imag * cos - real * sin).astype(bf16),
-            ]
-        moving = dot(jnp.concatenate(turned + back, 0), skew[...])
-        for s in range(2):
-            for half in range(order // lanes):
-                even = slice(half * lanes, (half + 1) * lanes)
-                odd = slice(order + half * lanes, order + (half + 1) * lanes)
-                real = moving[s * order : s * order + middle]
-                imag = moving[s * order + middle : (s + 1) * order]
-                put(s, 0, half, real[:, even] + imag[:, odd], real[:, even] - imag[:, odd])
-                put(s, 1, half, imag[:, even] - real[:, odd], -imag[:, even] - real[:, odd])
-                first = 2 * order + 2 * s * height
-                real = moving[first : first + height]
-                imag = moving[first + height : first + 2 * height]
-                fixed[s, 0, half] = real[:, even] - imag[:, odd]
-                fixed[s, 1, half] = -real[:, odd] - imag[:, even]
+            for i in range(height // NK):
+                real, imag = left[2 * i * NK : (2 * i + 1) * NK], left[(2 * i + 1) * NK : (2 * i + 2) * NK]
+                near = pl.ds(pl.multiple_of(group * height + i * NK, NK), NK)
+                cos, sin = unit[0, near], unit[1, near]
+                turned += [
+                    (cos * real + sin * imag).astype(bf16),
+                    (sin * real - cos * imag).astype(bf16),
+                ]
+        turned = jnp.concatenate(turned, 0)
+        for half in range(order // lanes):
+            moving = dot(turned, skew[half])
+            first = 0
+            for s in range(2):
+                for i in range(NW // 2):
+                    real, imag = moving[first : first + NK], moving[first + NK : first + 2 * NK]
+                    first += 2 * NK
+                    c, d, e, f = real[:, :lanes], real[:, lanes:], imag[:, :lanes], imag[:, lanes:]
+                    put(s, 0, half, i, c + f, c - f)
+                    put(s, 1, half, i, e - d, -e - d)
+                for i in range(height // NK):
+                    real, imag = moving[first : first + NK], moving[first + NK : first + 2 * NK]
+                    first += 2 * NK
+                    c, d, e, f = real[:, :lanes], real[:, lanes:], imag[:, :lanes], imag[:, lanes:]
+                    fixed[s, 0, half, i * NK : (i + 1) * NK] = c - f
+                    fixed[s, 1, half, i * NK : (i + 1) * NK] = -d - e
 
         @pl.loop(0, trans)
         def _(t):
@@ -513,7 +521,7 @@
             pltpu.VMEM((order, order), bf16),
             pltpu.VMEM((2 * height, order), bf16),
             pltpu.VMEM((2, order, order), f32),
-            pltpu.VMEM((order, 2 * order), bf16),
+            pltpu.VMEM((order // LANES, order, 2 * LANES), bf16),
             pltpu.VMEM((2, 2, order // LANES, NW, NK + ROWS, LANES), f32),
             pltpu.VMEM((2, 2, order // LANES, height, LANES), f32),
             pltpu.SMEM(shift_table.shape, jnp.int32),

time: 24.7 us -> 24.2 us (0.980)
  Pallas kernels: 23.9 us -> 23.4 us
    pallas_call x1, Pallas kernels: 22.3 us -> 21.9 us  [on_device(): pl.pallas_call(functools.partial(kernel, blocks, groups, reach), out_shap...]
where the time goes in v7:
time: 24.2 us; the launch traced here: 24.1 us
  Pallas kernels  23.4 us (97%)
  between operations  0.64 us (3%)
    pallas_call x1, Pallas kernels, on_device(): pl.pallas_call(functools.partial(kernel, blocks, groups, reach), out_shap...  21.9 us
    pallas_call x1, Pallas kernels, on_device(): pl.pallas_call(functools.partial(leave, groups), out_shape=(jax.ShapeDtyp...  1.54 us

profile of v7, /device:TPU:0, one launch (start us, length us, event | category | flops | bytes accessed | tf_op | source)
XLA Modules:
  0.0 24.1 jit_solution(144175580074700743)
XLA Ops:
  0.6 21.9 %shard_map.68 = (f32[4,4,2,64,128]{4,3,2,1,0:T(8,128)S(1)}, f32[2,4,64,256]{3,2,1,0:T(8,128)S(1)}, f32[2,4,64,256]{3,2,1,0:T(8,128)S(1)}) custom-call(s32[4,256]{1,0:T(4,128)} %table_ref.1, bf16[1,2,256,256]{3,2,1,0:T(8,128)(2,1)} %masses_ref.1, s32[1,256]{1,0:T(1,128)} %spins_ref.1, f32[2,4,64,256]{3,2,1,0:T(8,128)} %ph_ref.1, f32[2,4,64,256]{3,2,1,0:T(8,128)} %pp_ref.1), custom_call_target="tpu_custom_call" | custom-call | tf_op jit(solution)/shard_map/pallas_call | solution.py:509
  22.5 1.5 %shard_map.69 = (f32[2,4,64,256]{3,2,1,0:T(8,128)}, f32[2,4,64,256]{3,2,1,0:T(8,128)}) custom-call(f32[4,4,2,64,128]{4,3,2,1,0:T(8,128)S(1)} %get-tuple-element.5.sums, f32[2,4,64,256]{3,2,1,0:T(8,128)S(1)} %get-tuple-element.6.ph_keep, f32[2,4,64,256]{3,2,1,0:T(8,128)S(1)} %get-tuple-element.7.pp_keep), custom_call_target="tpu_custom_call" | custom-call | tf_op jit(solution)/shard_map/pallas_call | solution.py:536

commit v8 on v7

--- a/solution.py
+++ b/solution.py
@@ -44,7 +44,7 @@
 
 
 class Gather:
-    TURNS = ('', 'H0 O0 I0 O1', 'H1 h0 F0', 'F1 i0 I1', 'h1 f0', 'f1 i1', '', '')
+    TURNS = ('', 'H0 O0 I0 O1', 'H1 h0 F0 i0', 'F1 I1', 'h1 f0', 'f1 i1', '', '')
     SLOTS = 'SOHIFhfi'
 
     def __init__(self, group, block, order, walkers, masses, spins, held, held_spins, recv, sends):
@@ -473,20 +473,18 @@
     mom = (lane % NK - row % NK + NK) % NK
     source = freq * NK + mom
     index, upper = source % lanes, source >= lanes
-    copies = []
     for t in range(trans):
-        for keep, new, first in ((ph_keep, ph_new, 0), (pp_keep, pp_new, 2)):
+        for i, (keep, new, out) in enumerate(((ph_keep, ph_new, ph_out), (pp_keep, pp_new, pp_out))):
             for part in range(2):
                 low, high = [
-                    jnp.take_along_axis(sums[t, first + part, half], index, 1) for half in range(2)
+                    jnp.take_along_axis(sums[t, 2 * i + part, half], index, 1)
+                    for half in range(2)
                 ]
                 new[part, t, :, 0:lanes] = keep[part, t, :, 0:lanes] + jnp.where(upper, high, low)
                 new[part, t, :, lanes:] = keep[part, t, :, lanes:] + jnp.where(upper, low, high)
-        for i, (new, out) in enumerate(((ph_new, ph_out), (pp_new, pp_out))):
-            copies.append(pltpu.make_async_copy(new.at[:, t], out.at[:, t], sem.at[t, i]))
-            copies[-1].start()
-    for copy in copies:
-        copy.wait()
+                pltpu.make_async_copy(new.at[part, t], out.at[part, t], sem.at[i]).start()
+    for i, (new, out) in enumerate(((ph_new, ph_out), (pp_new, pp_out))):
+        pltpu.make_async_copy(new, out, sem.at[i]).wait()
 
 
 def on_device(masses, spins, shift_table, flip_table, ph_in, pp_in):
@@ -544,7 +542,7 @@
         scratch_shapes=[
             pltpu.VMEM(ph_in.shape, f32),
             pltpu.VMEM(pp_in.shape, f32),
-            dma((trans, 2)),
+            dma((2,)),
         ],
         compiler_params=pltpu.CompilerParams(vmem_limit_bytes=16 * 1024 * 1024),
     )(*[pltpu.with_memory_space_constraint(one, pltpu.VMEM) for one in sums])

time: 24.2 us -> 24.2 us (level)
  no operation moved by 1% of the time
where the time goes in v8:
time: 24.2 us; the launch traced here: 24.1 us
  Pallas kernels  23.5 us (97%)
  between operations  0.64 us (3%)
    pallas_call x1, Pallas kernels, on_device(): pl.pallas_call(functools.partial(kernel, blocks, groups, reach), out_shap...  22 us
    pallas_call x1, Pallas kernels, on_device(): pl.pallas_call(functools.partial(leave, groups), out_shape=(jax.ShapeDtyp...  1.46 us

profile of v8, /device:TPU:0, one launch (start us, length us, event | category | flops | bytes accessed | tf_op | source)
XLA Modules:
  0.0 24.1 jit_solution(2312210742979882476)
XLA Ops:
  0.6 22.0 %shard_map.68 = (f32[4,4,2,64,128]{4,3,2,1,0:T(8,128)S(1)}, f32[2,4,64,256]{3,2,1,0:T(8,128)S(1)}, f32[2,4,64,256]{3,2,1,0:T(8,128)S(1)}) custom-call(s32[4,256]{1,0:T(4,128)} %table_ref.1, bf16[1,2,256,256]{3,2,1,0:T(8,128)(2,1)} %masses_ref.1, s32[1,256]{1,0:T(1,128)} %spins_ref.1, f32[2,4,64,256]{3,2,1,0:T(8,128)} %ph_ref.1, f32[2,4,64,256]{3,2,1,0:T(8,128)} %pp_ref.1), custom_call_target="tpu_custom_call" | custom-call | tf_op jit(solution)/shard_map/pallas_call | solution.py:507
  22.6 1.5 %shard_map.69 = (f32[2,4,64,256]{3,2,1,0:T(8,128)}, f32[2,4,64,256]{3,2,1,0:T(8,128)}) custom-call(f32[4,4,2,64,128]{4,3,2,1,0:T(8,128)S(1)} %get-tuple-element.5.sums, f32[2,4,64,256]{3,2,1,0:T(8,128)S(1)} %get-tuple-element.6.ph_keep, f32[2,4,64,256]{3,2,1,0:T(8,128)S(1)} %get-tuple-element.7.pp_keep), custom_call_target="tpu_custom_call" | custom-call | tf_op jit(solution)/shard_map/pallas_call | solution.py:534

commit v9 on v8

--- a/solution.py
+++ b/solution.py
@@ -111,8 +111,8 @@
         send(src, dst, self.sends.at[0], self.recv.at[self.block, part], target).start()
 
     def note(self, target):
-        return send(self.spins, self.held_spins.at[self.block], self.sends.at[3],
-                    self.sends.at[4], target)
+        return send(self.spins, self.held_spins.at[self.block], self.sends.at[2],
+                    self.sends.at[3], target)
 
     def begin(self):
         for target in self.others():
@@ -157,7 +157,7 @@
             copy(1, part, self.beside).start()
         if kind in "HIhi" and part == 0:
             copy(1, 1, self.across).start()
-        copy(2, 2, self.partner).start()
+        copy(1, 2, self.partner).start()
 
     def some(self, count):
         return self.held.at[0:count, :, :, 0 : self.quarter]
@@ -172,7 +172,7 @@
 
         @pl.when(k == 1)
         def _():
-            bulk(self.held_spins.at[0:7], self.sends.at[4]).wait()
+            bulk(self.held_spins.at[0:7], self.sends.at[3]).wait()
 
         @pl.when(k >= 1)
         def _():
@@ -182,9 +182,8 @@
     def drain(self):
         pl.when(self.end)(lambda: bulk(self.some(7), self.sends.at[0]).wait())
         pl.when(jnp.logical_not(self.end))(lambda: bulk(self.some(5), self.sends.at[0]).wait())
-        bulk(self.some(8), self.sends.at[1]).wait()
-        bulk(self.held.at[0:7, :, :, 0 : 2 * self.quarter], self.sends.at[2]).wait()
-        bulk(self.held_spins.at[0:7], self.sends.at[3]).wait()
+        bulk(self.held.at[:, :, :, 0 : 11 * self.quarter // 4], self.sends.at[1]).wait()
+        bulk(self.held_spins.at[0:7], self.sends.at[2]).wait()
 
 
 class Chain:
@@ -419,7 +418,7 @@
                     fixed[s, 0, half, i * NK : (i + 1) * NK] = c - f
                     fixed[s, 1, half, i * NK : (i + 1) * NK] = -d - e
 
-        @pl.loop(0, trans)
+        @pl.loop(0, trans, unroll=2)
         def _(t):
             start = shift_ref[t, 0]
             freq, mom = lax.shift_right_logical(start, BITS), start & (NK - 1)
@@ -501,7 +500,7 @@
     dma = pltpu.SemaphoreType.DMA
     anywhere = pl.BlockSpec(memory_space=pl.ANY)
     if whole_gather(blocks, groups, reach):
-        recv_shape, send_shape = (visits, 3), (5,)
+        recv_shape, send_shape = (visits, 3), (4,)
     else:
         recv_shape, send_shape = (visits, groups + 1), (visits, 3 + 2 * (chips - 1))
     sums = pl.pallas_call(

time: 24.2 us -> 24.1 us (level)
  no operation moved by 1% of the time
where the time goes in v9:
time: 24.1 us; the launch traced here: 23.9 us
  Pallas kernels  23.3 us (97%)
  between operations  0.64 us (3%)
    pallas_call x1, Pallas kernels, on_device(): pl.pallas_call(functools.partial(kernel, blocks, groups, reach), out_shap...  21.8 us
    pallas_call x1, Pallas kernels, on_device(): pl.pallas_call(functools.partial(leave, groups), out_shape=(jax.ShapeDtyp...  1.46 us

profile of v9, /device:TPU:0, one launch (start us, length us, event | category | flops | bytes accessed | tf_op | source)
XLA Modules:
  0.0 23.9 jit_solution(4311784396861951522)
XLA Ops:
  0.6 21.8 %shard_map.68 = (f32[4,4,2,64,128]{4,3,2,1,0:T(8,128)S(1)}, f32[2,4,64,256]{3,2,1,0:T(8,128)S(1)}, f32[2,4,64,256]{3,2,1,0:T(8,128)S(1)}) custom-call(s32[4,256]{1,0:T(4,128)} %table_ref.1, bf16[1,2,256,256]{3,2,1,0:T(8,128)(2,1)} %masses_ref.1, s32[1,256]{1,0:T(1,128)} %spins_ref.1, f32[2,4,64,256]{3,2,1,0:T(8,128)} %ph_ref.1, f32[2,4,64,256]{3,2,1,0:T(8,128)} %pp_ref.1), custom_call_target="tpu_custom_call" | custom-call | tf_op jit(solution)/shard_map/pallas_call | solution.py:506
  22.4 1.5 %shard_map.69 = (f32[2,4,64,256]{3,2,1,0:T(8,128)}, f32[2,4,64,256]{3,2,1,0:T(8,128)}) custom-call(f32[4,4,2,64,128]{4,3,2,1,0:T(8,128)S(1)} %get-tuple-element.5.sums, f32[2,4,64,256]{3,2,1,0:T(8,128)S(1)} %get-tuple-element.6.ph_keep, f32[2,4,64,256]{3,2,1,0:T(8,128)S(1)} %get-tuple-element.7.pp_keep), custom_call_target="tpu_custom_call" | custom-call | tf_op jit(solution)/shard_map/pallas_call | solution.py:533

commit v10 on v8

--- a/solution.py
+++ b/solution.py
@@ -93,7 +93,7 @@
 
     def greet(self):
         self.barrier = pltpu.get_barrier_semaphore()
-        targets = self.others() + [self.partner, self.across]
+        targets = [self.across] + self.others()[::-1] + [self.partner]
         for target in targets:
             pl.semaphore_signal(self.barrier, inc=1, device_id=target, device_id_type=MESH)
 

time: 24.2 us -> 24.2 us (level)
  no operation moved by 1% of the time
where the time goes in v10:
time: 24.2 us; the launch traced here: 24 us
  Pallas kernels  23.3 us (96%)
  between operations  0.64 us (3%)
    pallas_call x1, Pallas kernels, on_device(): pl.pallas_call(functools.partial(kernel, blocks, groups, reach), out_shap...  21.9 us
    pallas_call x1, Pallas kernels, on_device(): pl.pallas_call(functools.partial(leave, groups), out_shape=(jax.ShapeDtyp...  1.46 us

profile of v10, /device:TPU:0, one launch (start us, length us, event | category | flops | bytes accessed | tf_op | source)
XLA Modules:
  0.0 24.0 jit_solution(15606601553222963713)
XLA Ops:
  0.6 21.9 %shard_map.68 = (f32[4,4,2,64,128]{4,3,2,1,0:T(8,128)S(1)}, f32[2,4,64,256]{3,2,1,0:T(8,128)S(1)}, f32[2,4,64,256]{3,2,1,0:T(8,128)S(1)}) custom-call(s32[4,256]{1,0:T(4,128)} %table_ref.1, bf16[1,2,256,256]{3,2,1,0:T(8,128)(2,1)} %masses_ref.1, s32[1,256]{1,0:T(1,128)} %spins_ref.1, f32[2,4,64,256]{3,2,1,0:T(8,128)} %ph_ref.1, f32[2,4,64,256]{3,2,1,0:T(8,128)} %pp_ref.1), custom_call_target="tpu_custom_call" | custom-call | tf_op jit(solution)/shard_map/pallas_call | solution.py:507
  22.5 1.5 %shard_map.69 = (f32[2,4,64,256]{3,2,1,0:T(8,128)}, f32[2,4,64,256]{3,2,1,0:T(8,128)}) custom-call(f32[4,4,2,64,128]{4,3,2,1,0:T(8,128)S(1)} %get-tuple-element.5.sums, f32[2,4,64,256]{3,2,1,0:T(8,128)S(1)} %get-tuple-element.6.ph_keep, f32[2,4,64,256]{3,2,1,0:T(8,128)S(1)} %get-tuple-element.7.pp_keep), custom_call_target="tpu_custom_call" | custom-call | tf_op jit(solution)/shard_map/pallas_call | solution.py:534
